TPU v7x, 256 devices: a whole 4x4x8 slice. The times are simulated.
256 devices in a mesh: seq: 64 (over z, y, core), round: 4 (over x).
Axes of the slice: x: 4, y: 4, z: 8, core: 2. Of those that a mesh axis runs over, the one named last changes fastest.
Arguments:
- queries: bfloat16 [16384, 1024], P('seq'), may hold values from -33 to 33
- keys: bfloat16 [16384, 1024], P('seq'), may hold values from -5 to 5
- values: bfloat16 [16384, 1024], P('seq'), may hold values from -6 to 6
- cotangent: bfloat16 [16384, 1024], P('seq'), may hold values from -6 to 6
- order: int32 [4, 16384], P('round', 'seq'), may hold values from 0 to 16383, as said below
- inverse: int32 [4, 16384], P('round', 'seq'), may hold values from 0 to 16383, as said below
- bucket: int32 [4, 16384], P('round'), may hold values from 0 to 63, as said below
Outputs:
- attended: bfloat16 [16384, 1024], P('seq')
- grad_queries: bfloat16 [16384, 1024], P('seq', 'round')
- grad_keys: bfloat16 [16384, 1024], P('seq', 'round')
- grad_values: bfloat16 [16384, 1024], P('seq', 'round')
Inputs may be any that keep to these rules, and one draw needn't show every extreme that they name: For each round, order lists every token once. In each round the tokens of one index of seq (256 consecutive rows) take at most 6 of the sorted positions of any one index of seq, and every index of seq sends exactly 6 of its tokens to some index of seq. inverse[r, order[r, j]] = j. Along a round's sorted positions the bucket numbers never fall, except that a last run of 1 to 128 positions at the end of the sequence carries bucket 0, the bucket of the first position.
All inputs are finite; a program needn't handle non-finite values.
Results may differ from a plain program's by a relative error of at most 0.014.
Values may be sent and summed in bfloat16 or wider, within the bound.
A program may use at most 64 MiB of HBM per device.

v0:
```python
import jax
import jax.numpy as jnp
from jax import lax
from jax.sharding import PartitionSpec as P

HEADS = 8
HEAD_DIM = 128
SPAN = 128


NEG = -1e30


def shifted(block, axis, distance):
    devices = range(lax.axis_size(axis))
    route = [((i - distance) % len(devices), i) for i in devices]
    return lax.ppermute(block, axis, route)


def combined_all(part, axis, combine):
    gathered = jax.tree.map(lambda a: lax.all_gather(a, axis), part)

    def take(source):
        return jax.tree.map(lambda a: lax.dynamic_index_in_dim(a, source, 0, False), gathered)

    return lax.fori_loop(
        1, lax.axis_size(axis), lambda source, state: combine(state, take(source)), take(0)
    )


def place_rows(rows, index, total):
    return jnp.zeros((total,) + rows.shape[1:], rows.dtype).at[index].set(rows)


def with_previous(blocks, previous):
    earlier = jnp.concatenate([previous[None], blocks[:-1]], axis=0)
    return jnp.concatenate([earlier, blocks], axis=1)


def split_heads(rows, blocks):
    return rows.reshape(blocks, rows.shape[0] // blocks, HEADS, HEAD_DIM)


def send_places(target, slots):
    counter = jnp.arange(target.shape[0], dtype=jnp.int32)
    before = counter[None, :] < counter[:, None]
    send_rank = jnp.sum((before & (target[:, None] == target[None, :])).astype(jnp.int32), axis=1)
    return target * slots + send_rank


def join_rounds(first, second):
    logsum_a, output_a = first
    logsum_b, output_b = second
    top = jnp.maximum(logsum_a, logsum_b)
    weight_a = jnp.exp(logsum_a - top)
    weight_b = jnp.exp(logsum_b - top)
    total = weight_a + weight_b
    rows = output_a.shape[0]
    mixed = (
        output_a.reshape(rows, HEADS, HEAD_DIM) * weight_a[..., None]
        + output_b.reshape(rows, HEADS, HEAD_DIM) * weight_b[..., None]
    ) / total[..., None]
    return (top + jnp.log(total), mixed.reshape(rows, HEADS * HEAD_DIM))


def on_device(queries, keys, values, cotangent, order, inverse, bucket):
    devices = lax.axis_size("seq")
    place = lax.axis_index("seq")
    tok_dev = queries.shape[0]
    feats = queries.shape[1]
    slots = 3 * tok_dev // (2 * devices)
    total_rows = devices * slots
    blocks = tok_dev // SPAN
    seq_len = bucket.shape[1]
    scale = HEAD_DIM ** (-0.5)
    f32 = jnp.float32
    sorted_tokens = order[0]
    send_index = send_places(inverse[0] // tok_dev, slots)
    source = sorted_tokens // tok_dev
    lower = sorted_tokens[None, :] < sorted_tokens[:, None]
    recv_rank = jnp.sum((lower & (source[:, None] == source[None, :])).astype(jnp.int32), axis=1)
    recv_index = source * slots + recv_rank
    packed = place_rows(
        jnp.concatenate([queries, keys, values, cotangent], axis=1), send_index, total_rows
    )
    arrived = lax.all_to_all(packed, "seq", split_axis=0, concat_axis=0, tiled=True)[recv_index]
    grad_sorted = arrived[:, 3 * feats :]
    query_sorted = arrived[:, :feats]
    key_sorted = arrived[:, feats : 2 * feats]
    value_sorted = arrived[:, 2 * feats : 3 * feats]
    tail = jnp.concatenate([key_sorted[-SPAN:], value_sorted[-SPAN:]], axis=1)
    tail_prev = shifted(tail, "seq", 1)
    query_heads = split_heads(query_sorted, blocks)
    key_window = with_previous(
        split_heads(key_sorted, blocks), split_heads(tail_prev[:, :feats], 1)[0]
    )
    value_window = with_previous(
        split_heads(value_sorted, blocks), split_heads(tail_prev[:, feats:], 1)[0]
    )
    my_bucket = lax.dynamic_slice_in_dim(bucket[0], place * tok_dev, tok_dev)
    prev_start = (place * tok_dev - SPAN + seq_len) % seq_len
    prev_bucket = lax.dynamic_slice_in_dim(bucket[0], prev_start, SPAN)
    query_bucket = my_bucket.reshape(blocks, SPAN)
    key_bucket = with_previous(query_bucket, prev_bucket)
    allowed = (query_bucket[:, :, None] == key_bucket[:, None, :])[:, None]
    scores = (
        jnp.einsum("cqhd,ckhd->chqk", query_heads, key_window, preferred_element_type=f32) * scale
    )
    peak = jnp.max(jnp.where(allowed, scores, NEG), axis=-1, keepdims=True)
    expon = jnp.exp(jnp.where(allowed, scores - peak, NEG))
    total = jnp.sum(expon, axis=-1, keepdims=True)
    weights = (expon / total).astype(jnp.bfloat16)
    output = jnp.einsum("chqk,ckhd->cqhd", weights, value_window, preferred_element_type=f32)
    output = output.reshape(tok_dev, feats)
    logsum = jnp.transpose((peak + jnp.log(total))[..., 0], (0, 2, 1)).reshape(tok_dev, HEADS)
    back = (
        lax.all_to_all(
            place_rows(output, recv_index, total_rows),
            "seq",
            split_axis=0,
            concat_axis=0,
            tiled=True,
        ),
        lax.all_to_all(
            place_rows(logsum, recv_index, total_rows),
            "seq",
            split_axis=0,
            concat_axis=0,
            tiled=True,
        ),
    )
    round_out = back[0][send_index]
    round_lse = back[1][send_index]
    merged_lse, combined = combined_all((round_lse, round_out), "round", join_rounds)
    attended = combined.astype(jnp.bfloat16)
    delta = jnp.sum(
        cotangent.reshape(tok_dev, HEADS, HEAD_DIM) * combined.reshape(tok_dev, HEADS, HEAD_DIM),
        axis=-1,
    )
    stats = (
        lax.all_to_all(
            place_rows(merged_lse, send_index, total_rows),
            "seq",
            split_axis=0,
            concat_axis=0,
            tiled=True,
        ),
        lax.all_to_all(
            place_rows(delta, send_index, total_rows),
            "seq",
            split_axis=0,
            concat_axis=0,
            tiled=True,
        ),
    )
    lse_sorted = stats[0][recv_index]
    delta_sorted = stats[1][recv_index]
    grad_heads = split_heads(grad_sorted, blocks)
    lse_block = jnp.transpose(lse_sorted.reshape(blocks, SPAN, HEADS), (0, 2, 1))[..., None]
    delta_block = jnp.transpose(delta_sorted.reshape(blocks, SPAN, HEADS), (0, 2, 1))[..., None]
    prob = jnp.exp(jnp.where(allowed, scores - lse_block, NEG))
    prob_low = prob.astype(jnp.bfloat16)
    value_grad = jnp.einsum("chqk,cqhd->ckhd", prob_low, grad_heads, preferred_element_type=f32)
    prob_grad = jnp.einsum("cqhd,ckhd->chqk", grad_heads, value_window, preferred_element_type=f32)
    score_grad = (prob * (prob_grad - delta_block)).astype(jnp.bfloat16)
    query_grad = (
        jnp.einsum("chqk,ckhd->cqhd", score_grad, key_window, preferred_element_type=f32) * scale
    )
    key_grad = (
        jnp.einsum("chqk,cqhd->ckhd", score_grad, query_heads, preferred_element_type=f32) * scale
    )
    key_grad = key_grad.reshape(blocks, 2 * SPAN, feats)
    value_grad = value_grad.reshape(blocks, 2 * SPAN, feats)
    spill = (
        shifted(key_grad[0, :SPAN].astype(jnp.bfloat16), "seq", -1).astype(jnp.float32),
        shifted(value_grad[0, :SPAN].astype(jnp.bfloat16), "seq", -1).astype(jnp.float32),
    )
    key_total = key_grad[:, SPAN:] + jnp.concatenate([key_grad[1:, :SPAN], spill[0][None]], axis=0)
    value_total = value_grad[:, SPAN:] + jnp.concatenate(
        [value_grad[1:, :SPAN], spill[1][None]], axis=0
    )
    round_grads = jnp.concatenate(
        [
            query_grad.reshape(tok_dev, feats),
            key_total.reshape(tok_dev, feats),
            value_total.reshape(tok_dev, feats),
        ],
        axis=1,
    ).astype(jnp.bfloat16)
    returned = lax.all_to_all(
        place_rows(round_grads, recv_index, total_rows),
        "seq",
        split_axis=0,
        concat_axis=0,
        tiled=True,
    )[send_index]
    shares = (
        lax.psum_scatter(
            returned[:, :feats].astype(f32).astype(jnp.bfloat16),
            "round",
            scatter_dimension=1,
            tiled=True,
        ).astype(jnp.float32),
        lax.psum_scatter(
            returned[:, feats : 2 * feats].astype(f32).astype(jnp.bfloat16),
            "round",
            scatter_dimension=1,
            tiled=True,
        ).astype(jnp.float32),
        lax.psum_scatter(
            returned[:, 2 * feats :].astype(f32).astype(jnp.bfloat16),
            "round",
            scatter_dimension=1,
            tiled=True,
        ).astype(jnp.float32),
    )
    return (
        attended,
        shares[0].astype(jnp.bfloat16),
        shares[1].astype(jnp.bfloat16),
        shares[2].astype(jnp.bfloat16),
    )


def solution(mesh):
    return jax.shard_map(
        on_device,
        mesh=mesh,
        in_specs=(
            P("seq", None),
            P("seq", None),
            P("seq", None),
            P("seq", None),
            P("round", "seq"),
            P("round", "seq"),
            P("round", None),
        ),
        out_specs=(P("seq", None), P("seq", "round"), P("seq", "round"), P("seq", "round")),
        check_vma=False,
    )
```

profile of v0, /device:TPU:8, one launch (start us, length us, event | category | flops | bytes accessed | tf_op | source)
XLA Modules:
  0.0 531.4 jit_solution(14053488729306606523)
XLA Ops:
  9.9 1.0 convert_reduce_fusion.1
  11.8 5.6 %scatter_custom_fusion = bf16[384,4096]{1,0:T(8,128)(2,1)S(1)} fusion(s32[256]{0:T(256)S(1)} %bitcast.198, bf16[256,1024]{1,0:T(8,128)(2,1)} %param.12, bf16[]{:T(256)} %constant.119, bf16[256,1024]{1,0:T(8,128)(2,1)} %param.11, bf16[256,1024]{1,0:T(8,128)(2,1)} %param.10, bf16[256,1024]{1,0:T(8,128)(2,1)} %param.9, bf16[]{:T(256)} %constant.112.clone.1), kind=kCustom, calls=%fused_computation.21 | custom fusion | flops 8388608 | bytes 5242884 | tf_op jit(solution)/shard_map/scatter | solution.py:32
  17.4 2.9 all_to_all.48
  20.3 12.3 %all-to-all-start = ((bf16[64,6,4096]{2,1,0:T(8,128)(2,1)}), bf16[64,6,4096]{2,1,0:T(8,128)(2,1)}, u32[]{:S(2)}, u32[]{:S(2)}) async-start(bf16[64,6,4096]{2,1,0:T(8,128)(2,1)} %all_to_all.48), calls=%async_computation | async-start | bytes 8388608 | tf_op jit(solution)/shard_map/all_to_all | solution.py:86
  34.1 94.6 %all-to-all-done = bf16[64,6,4096]{2,1,0:T(8,128)(2,1)} async-done(((bf16[64,6,4096]{2,1,0:T(8,128)(2,1)}), bf16[64,6,4096]{2,1,0:T(8,128)(2,1)}, u32[]{:S(2)}, u32[]{:S(2)}) %all-to-all-start) | async-done | bytes 3145760 | tf_op jit(solution)/shard_map/all_to_all | solution.py:86
  128.8 4.2 all_to_all.50
  132.9 3.2 gather_fusion
  136.1 2.0 concatenate.45
  138.6 1.1 fusion.52
  141.5 1.0 slice_bitcast_fusion
  144.3 3.2 collective-permute-done
  147.5 1.1 fusion.54
  149.9 0.9 fusion.10
  151.2 1.0 convolution_bitcast_fusion
  152.6 2.0 scatter_custom_fusion.2
  154.6 1.5 all_to_all.54
  156.1 8.9 %all-to-all-start.2 = ((f32[64,6,1024]{2,1,0:T(8,128)}), f32[64,6,1024]{2,1,0:T(8,128)}, u32[]{:S(2)}, u32[]{:S(2)}) async-start(f32[64,6,1024]{2,1,0:T(8,128)} %all_to_all.54), calls=%async_computation.2 | async-start | bytes 4194304 | tf_op jit(solution)/shard_map/all_to_all | solution.py:117
  165.1 51.2 %all-to-all-done.2 = f32[64,6,1024]{2,1,0:T(8,128)} async-done(((f32[64,6,1024]{2,1,0:T(8,128)}), f32[64,6,1024]{2,1,0:T(8,128)}, u32[]{:S(2)}, u32[]{:S(2)}) %all-to-all-start.2) | async-done | bytes 1572896 | tf_op jit(solution)/shard_map/all_to_all | solution.py:117
  216.3 1.6 all_to_all.56
  217.9 2.0 gather_fusion.2
  220.1 1.2 scatter_custom_fusion.1
  221.4 1.1 copy.115
  222.5 5.4 %all-to-all-start.1 = ((f32[64,6,8]{1,2,0:T(8,128)}), f32[64,6,8]{1,2,0:T(8,128)S(1)}, u32[]{:S(2)}, u32[]{:S(2)}) async-start(f32[64,6,8]{1,2,0:T(8,128)} %copy.115), calls=%async_computation.1 | async-start | bytes 524288 | tf_op jit(solution)/shard_map/all_to_all | solution.py:124
  228.5 11.7 %all-to-all-done.1 = f32[64,6,8]{1,2,0:T(8,128)S(1)} async-done(((f32[64,6,8]{1,2,0:T(8,128)}), f32[64,6,8]{1,2,0:T(8,128)S(1)}, u32[]{:S(2)}, u32[]{:S(2)}) %all-to-all-start.1) | async-done | bytes 12320 | tf_op jit(solution)/shard_map/all_to_all | solution.py:124
  241.4 15.9 %all-gather = f32[1024,8]{1,0:T(8,128)S(1)} all-gather(f32[256,8]{1,0:T(8,128)S(1)} %gather_fusion.1), channel_id=2, replica_groups=mesh['seq'=64,'round'=4] {'round'}, dimensions={0}, use_global_device_ids=true | all-gather | bytes 40960 | tf_op jit(solution)/shard_map/all_gather | solution.py:21
  257.5 13.8 %all-gather.4.cloned.1.call-done = f32[1024,1024]{1,0:T(8,128)} async-done(((f32[256,1024]{1,0:T(8,128)}), f32[1024,1024]{1,0:T(8,128)}) %all-gather.4.cloned.1.call-update) | async-done | bytes 4194320 | tf_op jit(solution)/shard_map/all_gather | solution.py:21
  271.4 1.3 slice.114
  272.7 11.2 %while.17 = (s32[]{:T(128)}, f32[256,8]{0,1:T(8,128)S(1)}, f32[256,1024]{1,0:T(8,128)S(1)}, f32[4,256,8]{1,2,0:T(8,128)S(1)}, f32[4,256,1024]{2,1,0:T(8,128)}, /*index=5*/s32[]{:T(128)}, s32[]{:T(128)}, s32[]{:T(128)}) while((s32[]{:T(128)}, f32[256,8]{0,1:T(8,128)S(1)}, f32[256,1024]{1,0:T(8,128)S(1)}, f32[4,256,8]{1,2,0:T(8,128)S(1)}, ...), condition=%wide.region_8.9_spmd, body=%wide.region_7.8_spmd.sunk | while | flops 1058821 | bytes 9560191 | solution.py:26
  274.1 2.3 bitcast_divide_fusion.2
  277.8 2.3 bitcast_divide_fusion.2
  281.5 2.3 bitcast_divide_fusion.2
  284.0 1.2 scatter_custom_fusion.3
  285.2 1.2 copy.126
  286.4 10.6 %all-to-all-start.3 = ((f32[64,6,8]{1,2,0:T(8,128)}), f32[64,6,8]{1,2,0:T(8,128)S(1)}, u32[]{:S(2)}, u32[]{:S(2)}) async-start(f32[64,6,8]{1,2,0:T(8,128)} %copy.126), calls=%async_computation.3 | async-start | bytes 524288 | tf_op jit(solution)/shard_map/all_to_all | solution.py:141
  296.9 1.0 multiply_bitcast_fusion
  298.5 1.2 scatter_custom_fusion.4
  299.8 1.2 copy.133
  300.9 8.2 %all-to-all-done.3 = f32[64,6,8]{1,2,0:T(8,128)S(1)} async-done(((f32[64,6,8]{1,2,0:T(8,128)}), f32[64,6,8]{1,2,0:T(8,128)S(1)}, u32[]{:S(2)}, u32[]{:S(2)}) %all-to-all-start.3) | async-done | bytes 12320 | tf_op jit(solution)/shard_map/all_to_all | solution.py:141
  309.2 6.0 %all-to-all-start.4 = ((f32[64,6,8]{1,2,0:T(8,128)}), f32[64,6,8]{1,2,0:T(8,128)}, u32[]{:S(2)}, u32[]{:S(2)}) async-start(f32[64,6,8]{1,2,0:T(8,128)} %copy.133), calls=%async_computation.4 | async-start | bytes 524288 | tf_op jit(solution)/shard_map/all_to_all | solution.py:148
  316.5 1.0 fusion.22
  318.2 0.8 slice.120
  319.2 8.3 %all-to-all-done.4 = f32[64,6,8]{1,2,0:T(8,128)} async-done(((f32[64,6,8]{1,2,0:T(8,128)}), f32[64,6,8]{1,2,0:T(8,128)}, u32[]{:S(2)}, u32[]{:S(2)}) %all-to-all-start.4) | async-done | bytes 12320 | tf_op jit(solution)/shard_map/all_to_all | solution.py:148
  327.4 2.1 copy.157
  329.5 1.0 reshape.446
  331.3 2.3 multiply_convert_fusion
  334.8 0.9 slice.117
  335.8 1.9 copy.166
  337.7 1.0 collective-permute-start.2
  338.7 2.5 fusion.20
  341.2 1.3 copy.138
  342.6 0.9 copy.185
  343.8 2.0 copy.165
  345.8 1.8 copy.163
  348.5 2.1 copy.162
  350.6 1.0 bitcast_convert_fusion
  352.9 4.7 scatter_custom_fusion.5
  357.5 2.8 all_to_all.63
  360.3 82.9 %all_to_all.72 = bf16[64,6,3072]{2,1,0:T(8,128)(2,1)} all-to-all(bf16[64,6,3072]{2,1,0:T(8,128)(2,1)S(1)} %all_to_all.63), channel_id=1, replica_groups=mesh['seq'=64,'round'=4] {'seq'}, dimensions={0} | all-to-all | bytes 4718592 | tf_op jit(solution)/shard_map/all_to_all | solution.py:190
  443.2 3.0 all_to_all.65
  446.2 2.7 gather_fusion.5
  448.9 2.6 fusion.53
  452.8 18.2 %reduce-scatter.8.cloned.1.call-done = bf16[256,256]{1,0:T(8,128)(2,1)} async-done(((bf16[256,1024]{1,0:T(8,128)(2,1)}), bf16[256,256]{1,0:T(8,128)(2,1)}) %reduce-scatter.8.cloned.1.call-update) | async-done | bytes 131088 | tf_op jit(solution)/shard_map/reduce_scatter | solution.py:210
  471.1 26.9 %reduce-scatter.6.cloned.1.call-done = bf16[256,256]{1,0:T(8,128)(2,1)} async-done(((bf16[256,1024]{1,0:T(8,128)(2,1)}), bf16[256,256]{1,0:T(8,128)(2,1)}) %reduce-scatter.6.cloned.1.call-update) | async-done | bytes 131088 | tf_op jit(solution)/shard_map/reduce_scatter | solution.py:204
  498.0 26.7 %reduce-scatter.4.cloned.1.call-done = bf16[256,256]{1,0:T(8,128)(2,1)} async-done(((bf16[256,1024]{1,0:T(8,128)(2,1)}), bf16[256,256]{1,0:T(8,128)(2,1)}) %reduce-scatter.4.cloned.1.call-update) | async-done | bytes 131088 | tf_op jit(solution)/shard_map/reduce_scatter | solution.py:198
  (131 shorter events, 26.1 us)
Async XLA Ops:
  11.8 208.3 %copy-start.19 = (s32[256,1]{0,1:T(1,128)}, s32[256,1]{0,1:T(1,128)S(1)}, u32[]{:S(2)}) copy-start(s32[256,1]{0,1:T(1,128)S(1)} %get-tuple-element.191) | copy-start | bytes 3076
  20.3 108.4 %all-to-all-start = ((bf16[64,6,4096]{2,1,0:T(8,128)(2,1)}), bf16[64,6,4096]{2,1,0:T(8,128)(2,1)}, u32[]{:S(2)}, u32[]{:S(2)}) async-start(bf16[64,6,4096]{2,1,0:T(8,128)(2,1)} %all_to_all.48), calls=%async_computation | async-start | bytes 8388608 | tf_op jit(solution)/shard_map/all_to_all | solution.py:86
  136.1 5.4 %copy-start = (bf16[256,4096]{1,0:T(8,128)(2,1)S(1)}, bf16[256,4096]{1,0:T(8,128)(2,1)}, u32[]{:S(2)}) copy-start(bf16[256,4096]{1,0:T(8,128)(2,1)} %gather_fusion) | copy-start | bytes 6291460
  138.1 9.4 %collective-permute-start = (bf16[128,2048]{1,0:T(8,128)(2,1)}, bf16[128,2048]{1,0:T(8,128)(2,1)}, u32[]{:S(2)}, u32[]{:S(2)}) collective-permute-start(bf16[128,2048]{1,0:T(8,128)(2,1)} %concatenate.45), channel_id=1, source_target_pairs={{252,0},{0,4},{4,8},{8,12},{12,16},{16,20},{20,24},{24,28},{28,32}... | collective-permute-start | bytes 1572872 | tf_op jit(solution)/shard_map/ppermute | solution.py:17
  142.5 1.0 copy-start.9
  143.0 7.7 %copy-start.14 = (bf16[2,128,8,128]{1,3,2,0:T(8,128)(2,1)}, bf16[2,128,8,128]{1,3,2,0:T(8,128)(2,1)S(1)}, u32[]{:S(2)}) copy-start(bf16[2,128,8,128]{1,3,2,0:T(8,128)(2,1)S(1)} %copy.120) | copy-start | bytes 1572868
  143.8 5.4 %copy-start.13 = (bf16[2,128,8,128]{3,1,2,0:T(8,128)(2,1)}, bf16[2,128,8,128]{3,1,2,0:T(8,128)(2,1)S(1)}, u32[]{:S(2)}) copy-start(bf16[2,128,8,128]{3,1,2,0:T(8,128)(2,1)S(1)} %copy.111) | copy-start | bytes 1572868
  143.9 5.3 copy-start.15
  144.3 5.5 %copy-start.3 = (bf16[2,128,8,128]{1,3,2,0:T(8,128)(2,1)}, bf16[2,128,8,128]{1,3,2,0:T(8,128)(2,1)S(1)}, u32[]{:S(2)}) copy-start(bf16[2,128,8,128]{1,3,2,0:T(8,128)(2,1)S(1)} %copy.139) | copy-start | bytes 1572868
  148.8 2.0 copy-start.18
  149.1 0.7 copy-start.17
  149.9 1.4 copy-start.1
  149.9 1.4 copy-start.16
  156.1 60.2 %all-to-all-start.2 = ((f32[64,6,1024]{2,1,0:T(8,128)}), f32[64,6,1024]{2,1,0:T(8,128)}, u32[]{:S(2)}, u32[]{:S(2)}) async-start(f32[64,6,1024]{2,1,0:T(8,128)} %all_to_all.54), calls=%async_computation.2 | async-start | bytes 4194304 | tf_op jit(solution)/shard_map/all_to_all | solution.py:117
  165.0 106.3 %all-gather.4.cloned.1.call-start = ((), (), s32[]{:S(2)}) async-start(), calls=%async_computation.12 | async-start | bytes 5242880 | tf_op jit(solution)/shard_map/all_gather | solution.py:21
  222.5 17.7 %all-to-all-start.1 = ((f32[64,6,8]{1,2,0:T(8,128)}), f32[64,6,8]{1,2,0:T(8,128)S(1)}, u32[]{:S(2)}, u32[]{:S(2)}) async-start(f32[64,6,8]{1,2,0:T(8,128)} %copy.115), calls=%async_computation.1 | async-start | bytes 524288 | tf_op jit(solution)/shard_map/all_to_all | solution.py:124
  228.4 88.1 %copy-start.5 = (bf16[2,128,8,128]{1,3,2,0:T(8,128)(2,1)}, bf16[2,128,8,128]{1,3,2,0:T(8,128)(2,1)S(1)}, u32[]{:S(2)}) copy-start(bf16[2,128,8,128]{1,3,2,0:T(8,128)(2,1)S(1)} %copy.143) | copy-start | bytes 1572868
  283.8 13.1 %copy-start.10 = (bf16[256,1024]{1,0:T(8,128)(2,1)S(1)}, bf16[256,1024]{1,0:T(8,128)(2,1)}, u32[]{:S(2)}) copy-start(bf16[256,1024]{1,0:T(8,128)(2,1)} %param.12) | copy-start | bytes 1572868
  286.4 22.8 %all-to-all-start.3 = ((f32[64,6,8]{1,2,0:T(8,128)}), f32[64,6,8]{1,2,0:T(8,128)S(1)}, u32[]{:S(2)}, u32[]{:S(2)}) async-start(f32[64,6,8]{1,2,0:T(8,128)} %copy.126), calls=%async_computation.3 | async-start | bytes 524288 | tf_op jit(solution)/shard_map/all_to_all | solution.py:141
  298.5 18.0 %copy-start.2 = (f32[2,8,128,256]{3,2,1,0:T(8,128)S(1)}, f32[2,8,128,256]{3,2,1,0:T(8,128)}, u32[]{:S(2)}) copy-start(f32[2,8,128,256]{3,2,1,0:T(8,128)} %copy-done.1) | copy-start | bytes 6291460
  309.2 18.3 %all-to-all-start.4 = ((f32[64,6,8]{1,2,0:T(8,128)}), f32[64,6,8]{1,2,0:T(8,128)}, u32[]{:S(2)}, u32[]{:S(2)}) async-start(f32[64,6,8]{1,2,0:T(8,128)} %copy.133), calls=%async_computation.4 | async-start | bytes 524288 | tf_op jit(solution)/shard_map/all_to_all | solution.py:148
  315.2 155.9 %reduce-scatter.8.cloned.1.call-start = ((), (), s32[]{:S(2)}) async-start(), calls=%async_computation.11 | async-start | bytes 655360 | tf_op jit(solution)/shard_map/reduce_scatter | solution.py:210
  331.3 2.4 copy-start.4
  333.7 1.2 copy-start.11
  335.7 3.0 copy-start.12
  337.7 12.9 %collective-permute-start.2 = (bf16[128,1024]{1,0:T(8,128)(2,1)}, bf16[128,1024]{1,0:T(8,128)(2,1)}, u32[]{:S(2)}, u32[]{:S(2)}) collective-permute-start(bf16[128,1024]{1,0:T(8,128)(2,1)} %bitcast.183), channel_id=1, source_target_pairs={{4,0},{8,4},{12,8},{16,12},{20,16},{24,20},{28,24},{32,28},{36,32}... | collective-permute-start | bytes 786440 | tf_op jit(solution)/shard_map/ppermute | solution.py:17
  347.6 4.7 collective-permute-start.1
  348.5 3.2 copy-start.7
  350.6 1.8 copy-start.8
  351.8 1.0 copy-start.6
  451.5 46.4 %reduce-scatter.6.cloned.1.call-start = ((), (), s32[]{:S(2)}) async-start(), calls=%async_computation.10 | async-start | bytes 655360 | tf_op jit(solution)/shard_map/reduce_scatter | solution.py:204
  452.3 72.4 %reduce-scatter.4.cloned.1.call-start = ((), (), s32[]{:S(2)}) async-start(), calls=%async_computation.9 | async-start | bytes 655360 | tf_op jit(solution)/shard_map/reduce_scatter | solution.py:198
Sparse Core Ops, SparseCore 0:
  220.1 51.2 all-gather.3
  451.6 19.3 reduce-scatter.7
  474.2 23.7 reduce-scatter.5
  500.9 23.7 reduce-scatter.3
where the time goes:
time: 539 us; the launch traced here: 531 us
  waiting for transfers between devices  265 us (49%)
  blocking collectives  98.7 us (18%)
  local copies, waits for them, and re-layouts  74.6 us (14%)
  starting transfers between devices  45.3 us (8%)
  other arithmetic  25.5 us (5%)
  between operations  14.6 us (3%)
  matrix products  7.76 us (1%)
    all_to_all x1, waiting for transfers between devices, on_device(): lax.all_to_all(packed, 'seq', split_axis=0, concat_axis=0, tiled=True)  94.6 us
    all_to_all x1, blocking collectives, on_device(): lax.all_to_all(place_rows(round_grads, recv_index, total_rows), 'seq', sp...  82.9 us
    all_to_all x1, waiting for transfers between devices, on_device(): lax.all_to_all(place_rows(output, recv_index, total_rows), 'seq', split_a...  51.2 us
    reduce_scatter x1, waiting for transfers between devices, on_device(): lax.psum_scatter(returned[:, feats:2 * feats].astype(f32).astype(jnp.bflo...  26.9 us
    reduce_scatter x1, waiting for transfers between devices, on_device(): lax.psum_scatter(returned[:, :feats].astype(f32).astype(jnp.bfloat16), 'r...  26.7 us
    reduce_scatter x1, waiting for transfers between devices, on_device(): lax.psum_scatter(returned[:, 2 * feats:].astype(f32).astype(jnp.bfloat16)...  18.2 us
    all_gather x1, blocking collectives, combined_all(): gathered = jax.tree.map(lambda a: lax.all_gather(a, axis), part)  15.9 us
    all_gather x1, waiting for transfers between devices, combined_all(): gathered = jax.tree.map(lambda a: lax.all_gather(a, axis), part)  13.8 us
  transfers between devices with their start and end apart: 12, of which 11 were waited for; matrix products, arithmetic and copies ran while one was open for 6% of the time, Pallas kernels for 0%

commit v1 on v0

v1 whole, which is shorter than its diff:
```python
import functools

import jax
import jax.numpy as jnp
from jax import lax
from jax.experimental import pallas as pl
from jax.experimental.pallas import tpu as pltpu
from jax.sharding import PartitionSpec as P

HEADS = 8
HEAD_DIM = 128
SPAN = 128
TOK = 256
SLOT = 6
GRP = 8
CHUNK = GRP * SLOT
MSG = GRP * CHUNK
ROUNDS = 4
ROWS = GRP * TOK
NBLK = ROWS // SPAN
NEG = -1e30
SCALE = HEAD_DIM ** (-0.5)
f32 = jnp.float32
bf16 = jnp.bfloat16
i32 = jnp.int32
ANY = pl.ANY


def here():
    x = lax.axis_index("round")
    s = lax.axis_index("seq")
    return x, lax.div(s, GRP), lax.rem(s, GRP)


def device(x, z, k):
    return {"seq": z * GRP + k, "round": x}


def remote(src, dst, send, recv, target):
    return pltpu.make_async_remote_copy(
        src_ref=src, dst_ref=dst, send_sem=send, recv_sem=recv,
        device_id=target, device_id_type=pl.DeviceIdType.MESH,
    )


def signal(sem, target):
    pl.semaphore_signal(sem, inc=1, device_id=target, device_id_type=pl.DeviceIdType.MESH)


def greet_line(barrier, x, z, k):
    me = x * GRP + z

    def go(i, c):
        o = lax.rem(me + i, 4 * GRP)
        signal(barrier, device(lax.div(o, GRP), lax.rem(o, GRP), k))
        return c

    lax.fori_loop(1, 4 * GRP, go, 0)


def greet_plane(barrier, x, z, k):
    me = x * GRP + k

    def go(i, c):
        o = lax.rem(me + i, 4 * GRP)
        signal(barrier, device(lax.div(o, GRP), z, lax.rem(o, GRP)))
        return c

    lax.fori_loop(1, 4 * GRP, go, 0)


def loop(lo, hi, body):
    def go(i, c):
        body(i)
        return c

    lax.fori_loop(lo, hi, go, 0)


def spread_kernel(q, k_, v, g, sidx, ridx, zin, sall, rall,
                  buf, zs, zr, ss, sr, rs, rr, ls):
    x, z, k = here()
    barrier = pltpu.get_barrier_semaphore()
    greet_line(barrier, x, z, k)
    mine = (z == k).astype(i32)

    def greet_pos(i):
        @pl.when(jnp.logical_or(z != k, i != z))
        def _():
            signal(barrier, device(x, i, z))

        @pl.when(jnp.logical_or(z != k, i != k))
        def _():
            signal(barrier, device(x, k, i))

    loop(0, GRP, greet_pos)
    pl.semaphore_wait(barrier, 4 * GRP - 1 + 2 * (GRP - mine))

    def cols(ref, h):
        return ref.at[:, pl.ds(pl.multiple_of(h * HEAD_DIM, HEAD_DIM), HEAD_DIM)]

    for t, ref in enumerate((q, k_, v, g)):
        @pl.when(x == t)
        def _(ref=ref):
            def go(i):
                o = lax.rem(z + i, GRP)
                remote(cols(ref, o), zin.at[z], zs.at[o], zr.at[z], device(x, o, k)).start()

            loop(1, GRP, go)
            pltpu.make_async_copy(cols(ref, z), buf, ls.at[0]).start()

    me = x * GRP + z

    def send_idx(i):
        o = lax.rem(me + i, 4 * GRP)
        remote(sidx, sall.at[me], ss.at[o], sr.at[me],
               device(lax.div(o, GRP), lax.rem(o, GRP), k)).start()

    loop(1, 4 * GRP, send_idx)
    pltpu.make_async_copy(sidx, sall.at[me], ls.at[1]).start()

    def send_pos(i):
        @pl.when(jnp.logical_or(z != k, i != z))
        def _():
            remote(ridx, rall.at[k], rs.at[i], rr.at[k], device(x, i, z)).start()

    loop(0, GRP, send_pos)

    @pl.when(z == k)
    def _():
        pltpu.make_async_copy(ridx, rall.at[k], ls.at[2]).start()
        pltpu.make_async_copy(ridx, rall.at[k], ls.at[2]).wait()

    pltpu.make_async_copy(cols(q, z), buf, ls.at[0]).wait()
    pltpu.make_async_copy(buf, zin.at[z], ls.at[3]).start()
    pltpu.make_async_copy(sidx, sall.at[me], ls.at[1]).wait()

    def wait_idx(i):
        o = lax.rem(me + i, 4 * GRP)
        cp = remote(sidx, sall.at[o], ss.at[o], sr.at[o],
                    device(lax.div(o, GRP), lax.rem(o, GRP), k))
        cp.wait_send()
        cp.wait_recv()

    loop(1, 4 * GRP, wait_idx)

    def wait_pos(i):
        @pl.when(jnp.logical_or(z != k, i != z))
        def _():
            remote(ridx, rall.at[k], rs.at[i], rr.at[i], device(x, i, z)).wait_send()

        @pl.when(jnp.logical_or(z != k, i != k))
        def _():
            remote(ridx, rall.at[i], rs.at[i], rr.at[i], device(x, k, i)).wait_recv()

    loop(0, GRP, wait_pos)

    def wait_rows(i):
        o = lax.rem(z + i, GRP)
        cp = remote(cols(q, o), zin.at[o], zs.at[o], zr.at[o], device(x, o, k))
        cp.wait_send()
        cp.wait_recv()

    loop(1, GRP, wait_rows)
    pltpu.make_async_copy(buf, zin.at[z], ls.at[3]).wait()


def spread(q, k, v, g, sidx, ridx):
    n = 4 * GRP
    return pl.pallas_call(
        spread_kernel,
        out_shape=(
            jax.ShapeDtypeStruct((GRP, TOK, HEAD_DIM), bf16),
            jax.ShapeDtypeStruct((n, 1, TOK), i32),
            jax.ShapeDtypeStruct((GRP, 1, TOK), i32),
        ),
        in_specs=[pl.BlockSpec(memory_space=ANY)] * 4 + [pl.BlockSpec(memory_space=pltpu.VMEM)] * 2,
        out_specs=(
            pl.BlockSpec(memory_space=ANY),
            pl.BlockSpec(memory_space=pltpu.VMEM),
            pl.BlockSpec(memory_space=pltpu.VMEM),
        ),
        scratch_shapes=[
            pltpu.VMEM((TOK, HEAD_DIM), bf16),
            pltpu.SemaphoreType.DMA((GRP,)),
            pltpu.SemaphoreType.DMA((GRP,)),
            pltpu.SemaphoreType.DMA((n,)),
            pltpu.SemaphoreType.DMA((n,)),
            pltpu.SemaphoreType.DMA((GRP,)),
            pltpu.SemaphoreType.DMA((GRP,)),
            pltpu.SemaphoreType.DMA((4,)),
        ],
        compiler_params=pltpu.CompilerParams(collective_id=0, has_side_effects=True),
        name="spread",
    )(q, k, v, g, sidx, ridx)


def plane_kernel(src, dst, buf, ss, rs, ls):
    x, z, k = here()
    me = x * GRP + k
    barrier = pltpu.get_barrier_semaphore()
    greet_plane(barrier, x, z, k)
    pl.semaphore_wait(barrier, 4 * GRP - 1)

    def other(i):
        o = lax.rem(me + i * 11, 4 * GRP)
        return o, device(lax.div(o, GRP), z, lax.rem(o, GRP))

    def go(i):
        o, target = other(i)
        remote(src.at[o], dst.at[me], ss.at[o], rs.at[me], target).start()

    loop(1, 4 * GRP, go)
    pltpu.make_async_copy(src.at[me], buf, ls.at[0]).start()
    pltpu.make_async_copy(src.at[me], buf, ls.at[0]).wait()
    pltpu.make_async_copy(buf, dst.at[me], ls.at[1]).start()

    def end(i):
        o, target = other(i)
        cp = remote(src.at[o], dst.at[o], ss.at[o], rs.at[o], target)
        cp.wait_send()
        cp.wait_recv()

    loop(1, 4 * GRP, end)
    pltpu.make_async_copy(buf, dst.at[me], ls.at[1]).wait()


def plane_exchange(packed, ident, name):
    return pl.pallas_call(
        plane_kernel,
        out_shape=jax.ShapeDtypeStruct(packed.shape, packed.dtype),
        in_specs=[pl.BlockSpec(memory_space=ANY)],
        out_specs=pl.BlockSpec(memory_space=ANY),
        scratch_shapes=[
            pltpu.VMEM(packed.shape[1:], packed.dtype),
            pltpu.SemaphoreType.DMA((4 * GRP,)),
            pltpu.SemaphoreType.DMA((4 * GRP,)),
            pltpu.SemaphoreType.DMA((2,)),
        ],
        compiler_params=pltpu.CompilerParams(collective_id=ident, has_side_effects=True),
        name=name,
    )(packed)


def row_onehot(idx, count):
    places = lax.broadcasted_iota(i32, (count, TOK), 0)
    return jnp.where(places == idx, 1.0, 0.0).astype(bf16)


def col_of(idx):
    wide = jnp.broadcast_to(idx.astype(f32), (128, TOK))
    return jnp.concatenate([wide[:, :128].T, wide[:, 128:].T], axis=0).astype(i32)


def col_onehot(idx, count):
    col = col_of(idx)
    lanes = lax.broadcasted_iota(i32, (TOK, 128), 1)
    parts = [jnp.where(col == lanes + m, 1.0, 0.0).astype(bf16) for m in range(0, count, 128)]
    return jnp.concatenate(parts, axis=1)


def dot(a, b):
    return jnp.dot(a, b, preferred_element_type=f32)


def dot_nt(a, b):
    return lax.dot_general(a, b, (((1,), (1,)), ((), ())), preferred_element_type=f32)


def dot_tn(a, b):
    return lax.dot_general(a, b, (((0,), (0,)), ((), ())), preferred_element_type=f32)


def pack_kernel(zin, sall, out):
    i = pl.program_id(0)
    for r in range(ROUNDS):
        onehot = row_onehot(sall[r * GRP + i], MSG)
        rows = dot(onehot, zin[0]).astype(bf16)
        out[r * GRP:(r + 1) * GRP, 0] = rows.reshape(GRP, CHUNK, HEAD_DIM)


def pack_tokens(zin, sall):
    return pl.pallas_call(
        pack_kernel,
        grid=(GRP,),
        out_shape=jax.ShapeDtypeStruct((4 * GRP, GRP, CHUNK, HEAD_DIM), bf16),
        in_specs=[
            pl.BlockSpec((1, TOK, HEAD_DIM), lambda i: (i, 0, 0)),
            pl.BlockSpec((4 * GRP, 1, TOK), lambda i: (0, 0, 0)),
        ],
        out_specs=pl.BlockSpec((4 * GRP, 1, CHUNK, HEAD_DIM), lambda i: (0, i, 0, 0)),
        name="pack_tokens",
    )(zin, sall)


def unpack_kernel(recv, swap, rall, rows, mid):
    def first(g):
        parts = [recv[t * GRP + g].reshape(MSG, HEAD_DIM) for t in range(4)]
        moved = dot(swap[...], jnp.concatenate(parts, axis=1)).astype(bf16)
        mid[:, g] = moved.reshape(GRP, CHUNK, 4 * HEAD_DIM)

    loop(0, GRP, first)

    def second(d):
        onehot = col_onehot(rall[d], MSG)
        rows[d] = dot(onehot, mid[d].reshape(MSG, 4 * HEAD_DIM)).astype(bf16)

    loop(0, GRP, second)


def unpack_rows(recv, swap, rall):
    return pl.pallas_call(
        unpack_kernel,
        out_shape=jax.ShapeDtypeStruct((GRP, TOK, 4 * HEAD_DIM), bf16),
        scratch_shapes=[pltpu.VMEM((GRP, GRP, CHUNK, 4 * HEAD_DIM), bf16)],
        name="unpack_rows",
    )(recv, swap, rall)


def allowed_of(bk, b):
    own = bk[b + 1]
    prev = bk[b]
    col = jnp.broadcast_to(own, (SPAN, SPAN)).T
    return jnp.concatenate([col == prev, col == own], axis=1)


def three(a):
    hi = a.astype(bf16)
    left = a - hi.astype(f32)
    mid = left.astype(bf16)
    low = (left - mid.astype(f32)).astype(bf16)
    return hi.astype(f32), mid.astype(f32), low.astype(f32)


def window(rows, tail, b):
    own = rows[b]
    before = jnp.where(b == 0, tail[...], rows[jnp.maximum(b - 1, 0)][:, HEAD_DIM:3 * HEAD_DIM])
    keys = jnp.concatenate([before[:, :HEAD_DIM], own[:, HEAD_DIM:2 * HEAD_DIM]], axis=0)
    vals = jnp.concatenate([before[:, HEAD_DIM:], own[:, 2 * HEAD_DIM:3 * HEAD_DIM]], axis=0)
    return own[:, :HEAD_DIM], keys, vals, own[:, 3 * HEAD_DIM:]


def forward_kernel(rows, tail, bk, swap, rall, out, stat, mid):
    lane = lax.rem(lax.broadcasted_iota(i32, (SPAN, 128), 1), 8)

    def block(b):
        query, keys, vals, grad = window(rows, tail, b)
        allowed = allowed_of(bk, b)
        scores = dot_nt(query, keys) * SCALE
        scores = jnp.where(allowed, scores, NEG)
        peak = jnp.max(scores, axis=-1, keepdims=True)
        expon = jnp.where(allowed, jnp.exp(scores - peak), 0.0)
        total = jnp.sum(expon, axis=-1, keepdims=True)
        weights = (expon / total).astype(bf16)
        output = dot(weights, vals)
        lse = peak + jnp.log(total)
        inner = jnp.sum(output * grad.astype(f32), axis=-1, keepdims=True)
        value = jnp.zeros((SPAN, 128), f32)
        for n, piece in enumerate(three(lse) + three(inner)):
            value = jnp.where(lane == n, piece, value)
        stat[b] = value.astype(bf16)

    loop(0, NBLK, block)
    group = lax.div(lax.broadcasted_iota(i32, (CHUNK, 128), 1), 8)

    def pack(d):
        onehot = row_onehot(rall[d], MSG)
        both = jnp.concatenate([stat[2 * d], stat[2 * d + 1]], axis=0)
        moved = dot(onehot, both)
        value = jnp.zeros((CHUNK, 128), f32)
        for g in range(GRP):
            value = jnp.where(group == g, moved[g * CHUNK:(g + 1) * CHUNK], value)
        mid[d] = value.astype(bf16)

    loop(0, GRP, pack)
    final = dot(swap[...], mid[...].reshape(MSG, 128))
    out[...] = final.T[:8 * GRP].reshape(GRP, 8, MSG)


def forward(rows, tail, bk, swap, rall):
    return pl.pallas_call(
        forward_kernel,
        out_shape=jax.ShapeDtypeStruct((GRP, 8, MSG), f32),
        scratch_shapes=[pltpu.VMEM((NBLK, SPAN, 128), bf16), pltpu.VMEM((GRP, CHUNK, 128), bf16)],
        name="forward",
    )(rows, tail, bk, swap, rall)


def stats_kernel(sent, sall, back, got, table, across, reply, s1, r1, s2, r2, s3, r3):
    x, z, k = here()
    barrier = pltpu.get_barrier_semaphore()

    def greet_k(i):
        signal(barrier, device(x, z, lax.rem(k + i, GRP)))

    def greet_x(i):
        signal(barrier, device(lax.rem(x + i, ROUNDS), z, k))

    loop(1, GRP, greet_k)
    loop(1, ROUNDS, greet_x)
    pl.semaphore_wait(barrier, GRP + ROUNDS - 2)

    def go1(i):
        o = lax.rem(k + i, GRP)
        remote(sent.at[o], got.at[k], s1.at[o], r1.at[k], device(x, z, o)).start()

    loop(1, GRP, go1)
    got[k] = sent[k]

    def fill(i):
        onehot = row_onehot(sall[x * GRP + i], MSG)
        table[:, i] = onehot.reshape(GRP, CHUNK, TOK)

    loop(0, GRP, fill)

    def end1(i):
        o = lax.rem(k + i, GRP)
        cp = remote(sent.at[o], got.at[o], s1.at[o], r1.at[o], device(x, z, o))
        cp.wait_send()
        cp.wait_recv()

    loop(1, GRP, end1)
    chunk_of = lax.broadcasted_iota(i32, (8, MSG), 1)
    row_of = lax.broadcasted_iota(i32, (8, MSG), 0)
    start = row_of * CHUNK
    keep = jnp.logical_and(chunk_of >= start, chunk_of < start + CHUNK)

    def collect(o, total):
        part = got[o]
        wide = [jnp.where(keep, jnp.broadcast_to(part[n:n + 1], (8, MSG)), 0.0) for n in range(6)]
        return total + dot(jnp.concatenate(wide, axis=0).astype(bf16), table[o].reshape(MSG, TOK))

    tok = lax.fori_loop(0, GRP, collect, jnp.zeros((48, TOK), f32))
    across[x, 0] = tok[0:8] + tok[8:16] + tok[16:24]
    across[x, 1] = tok[24:32] + tok[32:40] + tok[40:48]

    def go2(i):
        o = lax.rem(x + i, ROUNDS)
        remote(across.at[x], across.at[x], s2.at[o], r2.at[x], device(o, z, k)).start()

    loop(1, ROUNDS, go2)

    def end2(i):
        o = lax.rem(x + i, ROUNDS)
        cp = remote(across.at[x], across.at[o], s2.at[o], r2.at[o], device(o, z, k))
        cp.wait_send()
        cp.wait_recv()

    loop(1, ROUNDS, end2)
    lses = [across[r, 0] for r in range(ROUNDS)]
    top = jnp.maximum(jnp.maximum(lses[0], lses[1]), jnp.maximum(lses[2], lses[3]))
    exps = [jnp.exp(a - top) for a in lses]
    total = (exps[0] + exps[1]) + (exps[2] + exps[3])
    joint = top + jnp.log(total)
    delta = sum(exps[r] * across[r, 1] for r in range(ROUNDS)) / total
    pieces = jnp.concatenate(three(joint) + three(delta), axis=0).astype(bf16)

    def answer(o):
        wide = dot_nt(pieces, table[o].reshape(MSG, TOK))
        parts = [jnp.sum(jnp.where(keep, wide[n * 8:(n + 1) * 8], 0.0), axis=0, keepdims=True)
                 for n in range(6)]
        parts += [jnp.zeros((2, MSG), f32)]
        reply[o] = jnp.concatenate(parts, axis=0)

    loop(0, GRP, answer)

    def go3(i):
        o = lax.rem(k + i, GRP)
        remote(reply.at[o], back.at[k], s3.at[o], r3.at[k], device(x, z, o)).start()

    loop(1, GRP, go3)
    back[k] = reply[k]

    def end3(i):
        o = lax.rem(k + i, GRP)
        cp = remote(reply.at[o], back.at[o], s3.at[o], r3.at[o], device(x, z, o))
        cp.wait_send()
        cp.wait_recv()

    loop(1, GRP, end3)


def stats(sent, sall):
    dma = pltpu.SemaphoreType.DMA
    return pl.pallas_call(
        stats_kernel,
        out_shape=jax.ShapeDtypeStruct((GRP, 8, MSG), f32),
        in_specs=[pl.BlockSpec(memory_space=pltpu.VMEM)] * 2,
        out_specs=pl.BlockSpec(memory_space=pltpu.VMEM),
        scratch_shapes=[
            pltpu.VMEM((GRP, 8, MSG), f32),
            pltpu.VMEM((GRP, GRP, CHUNK, TOK), bf16),
            pltpu.VMEM((ROUNDS, 2, GRP, TOK), f32),
            pltpu.VMEM((GRP, 8, MSG), f32),
            dma((GRP,)), dma((GRP,)), dma((ROUNDS,)), dma((ROUNDS,)), dma((GRP,)), dma((GRP,)),
        ],
        compiler_params=pltpu.CompilerParams(collective_id=2, has_side_effects=True),
        name="stats",
    )(sent, sall)


def backward_kernel(rows, tail, bk, back, swap, rall, outq, outkv, mid):
    flat = back[...].reshape(8 * GRP, MSG)
    wide = jnp.concatenate([flat, jnp.zeros((128 - 8 * GRP, MSG), f32)], axis=0)
    mid[...] = dot(swap[...], wide.T.astype(bf16)).astype(bf16).reshape(GRP, CHUNK, 128)
    group = lax.div(lax.broadcasted_iota(i32, (CHUNK, 128), 1), 8)
    lane = lax.rem(lax.broadcasted_iota(i32, (TOK, 128), 1), 8)
    outkv[0] = jnp.zeros((SPAN, 2 * HEAD_DIM), f32)

    def body(d):
        part = mid[d].astype(f32)
        spread_rows = jnp.concatenate(
            [jnp.where(group == g, part, 0.0) for g in range(GRP)], axis=0
        ).astype(bf16)
        found = dot(col_onehot(rall[d], MSG), spread_rows)
        joint = jnp.sum(jnp.where(lane < 3, found, 0.0), axis=-1, keepdims=True)
        delta = jnp.sum(jnp.where(jnp.logical_and(lane >= 3, lane < 6), found, 0.0), axis=-1,
                        keepdims=True)
        for half in range(2):
            b = 2 * d + half
            query, keys, vals, grad = window(rows, tail, b)
            allowed = allowed_of(bk, b)
            scores = dot_nt(query, keys) * SCALE
            lse = joint[half * SPAN:(half + 1) * SPAN]
            prob = jnp.exp(jnp.where(allowed, scores - lse, NEG))
            low = prob.astype(bf16)
            value_grad = dot_tn(low, grad)
            prob_grad = dot_nt(grad, vals)
            score_grad = (prob * (prob_grad - delta[half * SPAN:(half + 1) * SPAN])).astype(bf16)
            query_grad = dot(score_grad, keys) * SCALE
            key_grad = dot_tn(score_grad, query) * SCALE
            outq[b] = jnp.concatenate([dot(low, vals), query_grad], axis=1).astype(bf16)
            both = jnp.concatenate([key_grad, value_grad], axis=1)
            outkv[b] = outkv[b] + both[:SPAN]
            outkv[b + 1] = both[SPAN:]

    loop(0, GRP, body)


def backward(rows, tail, bk, back, swap, rall):
    return pl.pallas_call(
        backward_kernel,
        out_shape=(
            jax.ShapeDtypeStruct((NBLK, SPAN, 2 * HEAD_DIM), bf16),
            jax.ShapeDtypeStruct((NBLK + 1, SPAN, 2 * HEAD_DIM), f32),
        ),
        scratch_shapes=[pltpu.VMEM((GRP, CHUNK, 128), bf16)],
        name="backward",
    )(rows, tail, bk, back, swap, rall)


def repack_kernel(zref, outq, outkv, spill, swap, rall, out, mid):
    z = zref[0]

    def first(d):
        onehot = row_onehot(rall[d], MSG)
        upper = jnp.concatenate([outq[2 * d], outkv[2 * d + 1].astype(bf16)], axis=1)
        last = outkv[2 * d + 2] + jnp.where(d == GRP - 1, spill[...].astype(f32), 0.0)
        lower = jnp.concatenate([outq[2 * d + 1], last.astype(bf16)], axis=1)
        moved = dot(onehot, jnp.concatenate([upper, lower], axis=0)).astype(bf16)
        mid[:, d] = moved.reshape(GRP, CHUNK, 4 * HEAD_DIM)

    loop(0, GRP, first)

    def second(g):
        moved = dot(swap[...], mid[g].reshape(MSG, 4 * HEAD_DIM)).astype(bf16)
        for i in range(GRP):
            for t in range(4):
                owner = lax.rem(t - i - z + 16, 4)
                out[owner * GRP + g, i] = moved[i * CHUNK:(i + 1) * CHUNK,
                                                t * HEAD_DIM:(t + 1) * HEAD_DIM]

    loop(0, GRP, second)


def repack(z, outq, outkv, spill, swap, rall):
    vm = pl.BlockSpec(memory_space=pltpu.VMEM)
    return pl.pallas_call(
        repack_kernel,
        out_shape=jax.ShapeDtypeStruct((4 * GRP, GRP, CHUNK, HEAD_DIM), bf16),
        in_specs=[pl.BlockSpec(memory_space=pltpu.SMEM), vm, vm, vm, vm, vm],
        out_specs=vm,
        scratch_shapes=[pltpu.VMEM((GRP, GRP, CHUNK, 4 * HEAD_DIM), bf16)],
        name="repack",
    )(z, outq, outkv, spill, swap, rall)


def settle_kernel(recv, sall, out):
    i = pl.program_id(0)
    total = jnp.zeros((TOK, HEAD_DIM), f32)
    for r in range(ROUNDS):
        onehot = col_onehot(sall[r * GRP + i], MSG)
        total = total + dot(onehot, recv[r * GRP:(r + 1) * GRP, 0].reshape(MSG, HEAD_DIM))
    out[0] = total.astype(bf16)


def settle(recv, sall):
    return pl.pallas_call(
        settle_kernel,
        grid=(GRP,),
        out_shape=jax.ShapeDtypeStruct((GRP, TOK, HEAD_DIM), bf16),
        in_specs=[
            pl.BlockSpec((4 * GRP, 1, CHUNK, HEAD_DIM), lambda i: (0, i, 0, 0)),
            pl.BlockSpec((4 * GRP, 1, TOK), lambda i: (0, 0, 0)),
        ],
        out_specs=pl.BlockSpec((1, TOK, HEAD_DIM), lambda i: (i, 0, 0)),
        name="settle",
    )(recv, sall)


def home_kernel(rows, att, gq, gk, gv, buf, ss, ra, rg, ls):
    x, z, k = here()
    barrier = pltpu.get_barrier_semaphore()
    greet_line(barrier, x, z, k)
    pl.semaphore_wait(barrier, 4 * GRP - 1)

    def tile(ref, h):
        return ref.at[:, pl.ds(pl.multiple_of(h * HEAD_DIM, HEAD_DIM), HEAD_DIM)]

    grads = (gq, gk, gv)
    owner = lax.div(z, 2)
    side = lax.rem(z, 2)

    def each(i, begin):
        kind = lax.rem(x + i + z, 4)

        @pl.when(kind == 0)
        def _():
            for o in range(ROUNDS):
                own = jnp.logical_and(x == o, z == i)

                @pl.when(jnp.logical_not(own))
                def _(o=o):
                    cp = remote(rows.at[i], tile(att, z), ss.at[i, o], ra.at[z], device(o, i, k))
                    cp.start() if begin else cp.wait_send()

                @pl.when(own)
                def _():
                    local(tile(att, z), begin)

        for t in range(3):
            own = jnp.logical_and(x == owner, z == i)

            @pl.when(jnp.logical_and(kind == t + 1, jnp.logical_not(own)))
            def _(t=t):
                cp = remote(rows.at[i], tile(grads[t], side), ss.at[i, 0], rg.at[2 * t + side],
                            device(owner, i, k))
                cp.start() if begin else cp.wait_send()

            @pl.when(jnp.logical_and(kind == t + 1, own))
            def _(t=t):
                local(tile(grads[t], side), begin)

    def local(dst, begin):
        if begin:
            pltpu.make_async_copy(rows.at[z], buf, ls.at[0]).start()
            pltpu.make_async_copy(rows.at[z], buf, ls.at[0]).wait()
            pltpu.make_async_copy(buf, dst, ls.at[1]).start()
        else:
            pltpu.make_async_copy(buf, dst, ls.at[1]).wait()

    loop(0, GRP, lambda i: each(lax.rem(z + i, GRP), True))
    loop(0, GRP, lambda i: each(lax.rem(z + i, GRP), False))

    def arrive_att(h):
        sender = lax.rem(32 - z - h, 4)

        @pl.when(jnp.logical_not(jnp.logical_and(h == z, sender == x)))
        def _():
            remote(rows.at[0], tile(att, h), ss.at[0, 0], ra.at[h], device(sender, h, k)).wait_recv()

    loop(0, GRP, arrive_att)
    for t in range(3):
        for n in range(2):
            h = 2 * x + n
            sender = lax.rem(32 + t + 1 - z - h, 4)

            @pl.when(jnp.logical_not(jnp.logical_and(h == z, sender == x)))
            def _(t=t, n=n, h=h, sender=sender):
                remote(rows.at[0], tile(grads[t], n), ss.at[0, 0], rg.at[2 * t + n],
                       device(sender, h, k)).wait_recv()


def home(rows):
    dma = pltpu.SemaphoreType.DMA
    part = jax.ShapeDtypeStruct((TOK, 2 * HEAD_DIM), bf16)
    return pl.pallas_call(
        home_kernel,
        out_shape=(jax.ShapeDtypeStruct((TOK, HEADS * HEAD_DIM), bf16), part, part, part),
        in_specs=[pl.BlockSpec(memory_space=ANY)],
        out_specs=(pl.BlockSpec(memory_space=ANY),) * 4,
        scratch_shapes=[
            pltpu.VMEM((TOK, HEAD_DIM), bf16),
            dma((GRP, ROUNDS)), dma((GRP,)), dma((6,)), dma((2,)),
        ],
        compiler_params=pltpu.CompilerParams(collective_id=4, has_side_effects=True),
        name="home",
    )(rows)


def ranked(group, before):
    same = group[:, None] == group[None, :]
    return jnp.sum(jnp.logical_and(before, same).astype(i32), axis=1)


def shift(rows, step):
    n = lax.axis_size("seq")
    route = [(i, i - i % GRP + (i % GRP + step) % GRP) for i in range(n)]
    return lax.ppermute(rows, "seq", route)


def on_device(queries, keys, values, cotangent, order, inverse, bucket):
    s = lax.axis_index("seq")
    k = s % GRP
    z = s // GRP
    tokens = order[0]
    target = inverse[0] // TOK
    counter = jnp.arange(TOK, dtype=i32)
    sidx = target * SLOT + ranked(target, counter[None, :] < counter[:, None])
    source = tokens // TOK
    rank = ranked(source, tokens[None, :] < tokens[:, None])
    ridx = (source % GRP) * CHUNK + (source // GRP) * SLOT + rank
    zin, sall, rall = spread(queries, keys, values, cotangent,
                             sidx.reshape(1, TOK), ridx.reshape(1, TOK))
    place = jnp.arange(MSG, dtype=i32)
    mirror = (place // SLOT % GRP) * CHUNK + (place // CHUNK) * SLOT + place % SLOT
    swap = (mirror[:, None] == place[None, :]).astype(bf16)
    seq_len = bucket.shape[1]
    near = jnp.concatenate([bucket[0, -SPAN:], bucket[0]])
    bk = lax.dynamic_slice_in_dim(near, k * ROWS, ROWS + SPAN).astype(f32)
    bk = bk.reshape(NBLK + 1, 1, SPAN)
    recv = plane_exchange(pack_tokens(zin, sall), 1, "plane_out")
    rows = unpack_rows(recv, swap, rall)
    rows = rows.reshape(NBLK, SPAN, 4 * HEAD_DIM)
    tail = shift(rows[NBLK - 1, :, HEAD_DIM:3 * HEAD_DIM], 1)
    back = stats(forward(rows, tail, bk, swap, rall), sall)
    outq, outkv = backward(rows, tail, bk, back, swap, rall)
    spill = shift(outkv[0].astype(bf16), -1)
    packed = repack(z.reshape(1), outq, outkv, spill, swap, rall)
    settled = settle(plane_exchange(packed, 3, "plane_back"), sall)
    return home(settled)


def solution(mesh):
    return jax.shard_map(
        on_device,
        mesh=mesh,
        in_specs=(
            P("seq", None), P("seq", None), P("seq", None), P("seq", None),
            P("round", "seq"), P("round", "seq"), P("round", None),
        ),
        out_specs=(P("seq", None), P("seq", "round"), P("seq", "round"), P("seq", "round")),
        check_vma=False,
    )
```

time: 539 us -> 252 us (0.47)
  the two profiles are of different devices: /device:TPU:8 before, /device:TPU:71 now
where the time goes in v1:
time: 252 us; the launch traced here: 248 us
  Pallas kernels  227 us (90%)
  local copies, waits for them, and re-layouts  10.2 us (4%)
  other arithmetic  6.12 us (2%)
  waiting for transfers between devices  3.91 us (2%)
    pallas_call x2, Pallas kernels, plane_exchange(): pl.pallas_call(plane_kernel, out_shape=jax.ShapeDtypeStruct(packed.shape,...  85.2 us
    pallas_call x1, Pallas kernels, home(): pl.pallas_call(home_kernel, out_shape=(jax.ShapeDtypeStruct((TOK, HEADS *...  36.4 us
    pallas_call x1, Pallas kernels, spread(): pl.pallas_call(spread_kernel, out_shape=(jax.ShapeDtypeStruct((GRP, TOK,...  25.7 us
    pallas_call x1, Pallas kernels, stats(): pl.pallas_call(stats_kernel, out_shape=jax.ShapeDtypeStruct((GRP, 8, MSG)...  23.1 us
    pallas_call x1, Pallas kernels, forward(): pl.pallas_call(forward_kernel, out_shape=jax.ShapeDtypeStruct((GRP, 8, MS...  13.5 us
    pallas_call x1, Pallas kernels, backward(): pl.pallas_call(backward_kernel, out_shape=(jax.ShapeDtypeStruct((NBLK, SP...  11.3 us
    pallas_call x1, Pallas kernels, unpack_rows(): pl.pallas_call(unpack_kernel, out_shape=jax.ShapeDtypeStruct((GRP, TOK, 4...  9.07 us
    pallas_call x1, Pallas kernels, repack(): pl.pallas_call(repack_kernel, out_shape=jax.ShapeDtypeStruct((4 * GRP, GR...  8.74 us
  transfers between devices with their start and end apart: 2, of which 2 were waited for; matrix products, arithmetic and copies ran while one was open for 0% of the time, Pallas kernels for 0%

profile of v1, /device:TPU:71, one launch (start us, length us, event | category | flops | bytes accessed | tf_op | source)
XLA Modules:
  0.0 248.2 jit_solution(17853595284303824418)
XLA Ops:
  0.7 0.7 and_select_fusion.3
  1.3 0.7 and_select_fusion.5
  2.0 0.7 and_select_fusion.2
  2.7 0.7 and_select_fusion.4
  3.4 0.8 fusion.swap
  4.2 1.0 convert_reduce_fusion
  5.2 0.2 convert_reduce_fusion.1
  5.4 1.3 fusion.20
  6.7 25.7 %spread.1 = (bf16[8,256,128]{2,1,0:T(8,128)(2,1)}, s32[32,1,256]{2,1,0:T(1,128)}, s32[8,1,256]{2,1,0:T(1,128)}) custom-call(bf16[256,1024]{1,0:T(8,128)(2,1)} %q.1, bf16[256,1024]{1,0:T(8,128)(2,1)} %k_.1, bf16[256,1024]{1,0:T(8,128)(2,1)} %v.1, bf16[256,1024]{1,0:T(8,128)(2,1)} %g.1, s32[1,256]{1,0:T(1,128)} %get-tuple-element.15.sidx, ...), custom_call_target="tpu_custom_call" | custom-call | tf_op jit(solution)/shard_map/spread/pallas_call | solution.py:170
  32.3 6.7 %pack_tokens.1.src = bf16[32,8,48,128]{3,2,1,0:T(8,128)(2,1)} custom-call(bf16[8,256,128]{2,1,0:T(8,128)(2,1)} %get-tuple-element.9.zin, s32[32,1,256]{2,1,0:T(1,128)} %get-tuple-element.10.sall), custom_call_target="tpu_custom_call" | custom-call | tf_op jit(solution)/shard_map/pack_tokens/pallas_call | solution.py:283
  39.0 43.0 %plane_out.1.recv = bf16[32,8,48,128]{3,2,1,0:T(8,128)(2,1)} custom-call(bf16[32,8,48,128]{3,2,1,0:T(8,128)(2,1)} %pack_tokens.1.src), custom_call_target="tpu_custom_call" | custom-call | tf_op jit(solution)/shard_map/plane_out/pallas_call | solution.py:229
  82.0 0.0 copy-start.2
  82.0 9.1 %unpack_rows.1 = bf16[8,256,512]{2,1,0:T(8,128)(2,1)} custom-call(bf16[32,8,48,128]{3,2,1,0:T(8,128)(2,1)} %plane_out.1.recv, bf16[384,384]{1,0:T(8,128)(2,1)} %fusion.swap, s32[8,1,256]{2,1,0:T(1,128)} %get-tuple-element.11.rall), custom_call_target="tpu_custom_call" | custom-call | tf_op jit(solution)/shard_map/unpack_rows/pallas_call | solution.py:312
  91.1 0.8 slice_bitcast_fusion
  91.9 0.0 collective-permute-start
  91.9 0.0 copy-done.2
  91.9 0.1 fusion.4
  92.0 0.6 reshape.121.bk
  92.7 0.6 collective-permute-done.tail
  93.3 0.0 copy-start
  93.3 0.6 copy-done
  93.9 13.5 %forward.1.sent = f32[8,8,384]{2,1,0:T(8,128)} custom-call(bf16[16,128,512]{2,1,0:T(8,128)(2,1)} %bitcast.16, bf16[128,256]{1,0:T(8,128)(2,1)} %copy-done, f32[17,1,128]{2,1,0:T(1,128)} %reshape.121.bk, bf16[384,384]{1,0:T(8,128)(2,1)} %fusion.swap, s32[8,1,256]{2,1,0:T(1,128)} %get-tuple-element.11.rall), custom_call_target="tpu_custom_call" | custom-call | tf_op jit(solution)/shard_map/forward/pallas_call | solution.py:381
  107.4 23.1 %stats.1.back = f32[8,8,384]{2,1,0:T(8,128)} custom-call(f32[8,8,384]{2,1,0:T(8,128)} %forward.1.sent, s32[32,1,256]{2,1,0:T(1,128)} %get-tuple-element.10.sall), custom_call_target="tpu_custom_call" | custom-call | tf_op jit(solution)/shard_map/stats/pallas_call | solution.py:485
  130.5 11.3 %backward.1 = (bf16[16,128,256]{2,1,0:T(8,128)(2,1)}, f32[17,128,256]{2,1,0:T(8,128)}) custom-call(bf16[16,128,512]{2,1,0:T(8,128)(2,1)} %bitcast.17, bf16[128,256]{1,0:T(8,128)(2,1)} %copy-done, f32[17,1,128]{2,1,0:T(1,128)} %reshape.121.bk, f32[8,8,384]{2,1,0:T(8,128)} %stats.1.back, bf16[384,384]{1,0:T(8,128)(2,1)} %fusion.swap, ...), custom_call_target="tpu_custom_call" | custom-call | tf_op jit(solution)/shard_map/backward/pallas_call | solution.py:541
  141.8 0.9 fusion.2
  142.7 0.4 collective-permute-start.1
  143.1 3.3 %collective-permute-done.1.spill = bf16[128,256]{1,0:T(8,128)(2,1)S(1)} collective-permute-done((bf16[128,256]{1,0:T(8,128)(2,1)S(1)}, bf16[128,256]{1,0:T(8,128)(2,1)S(1)}, u32[]{:S(2)}, u32[]{:S(2)}) %collective-permute-start.1) | collective-permute-done | bytes 65568 | tf_op jit(solution)/shard_map/ppermute | solution.py:709
  146.4 0.0 copy-start.1
  146.4 0.6 copy-done.1
  147.0 8.7 %repack.1.src = bf16[32,8,48,128]{3,2,1,0:T(8,128)(2,1)} custom-call(s32[1]{0:T(128)} %bitcast.zref, bf16[16,128,256]{2,1,0:T(8,128)(2,1)} %get-tuple-element.12.outq, f32[17,128,256]{2,1,0:T(8,128)} %get-tuple-element.13.outkv, bf16[128,256]{1,0:T(8,128)(2,1)} %copy-done.1, bf16[384,384]{1,0:T(8,128)(2,1)} %fusion.swap, s32[8,1,256]{2,1,0:T(1,128)} %get-tuple-element.11.rall), custom_call_target="tpu_custom_call" | custom-call | tf_op jit(solution)/shard_map/repack/pallas_call | solution.py:578
  155.7 42.3 %plane_back.1.recv = bf16[32,8,48,128]{3,2,1,0:T(8,128)(2,1)} custom-call(bf16[32,8,48,128]{3,2,1,0:T(8,128)(2,1)} %repack.1.src), custom_call_target="tpu_custom_call" | custom-call | tf_op jit(solution)/shard_map/plane_back/pallas_call | solution.py:229
  198.0 7.2 %settle.1.rows = bf16[8,256,128]{2,1,0:T(8,128)(2,1)} custom-call(bf16[32,8,48,128]{3,2,1,0:T(8,128)(2,1)} %plane_back.1.recv, s32[32,1,256]{2,1,0:T(1,128)} %get-tuple-element.10.sall), custom_call_target="tpu_custom_call" | custom-call | tf_op jit(solution)/shard_map/settle/pallas_call | solution.py:598
  205.2 36.4 %home.1 = (bf16[256,1024]{1,0:T(8,128)(2,1)}, bf16[256,256]{1,0:T(8,128)(2,1)}, bf16[256,256]{1,0:T(8,128)(2,1)}, bf16[256,256]{1,0:T(8,128)(2,1)}) custom-call(bf16[8,256,128]{2,1,0:T(8,128)(2,1)} %settle.1.rows), custom_call_target="tpu_custom_call" | custom-call | tf_op jit(solution)/shard_map/home/pallas_call | solution.py:687
  241.6 1.9 copy.15
  243.5 1.6 copy.16
  245.1 1.6 copy.17
  246.6 1.6 copy.18
  (2 shorter events, 0.0 us)
Async XLA Ops:
  82.0 9.9 %copy-start.2 = (s32[1,16384]{1,0:T(1,128)S(1)}, s32[1,16384]{1,0:T(1,128)}, u32[]{:S(2)}) copy-start(s32[1,16384]{1,0:T(1,128)} %param.13) | copy-start | bytes 196612
  91.9 1.3 collective-permute-start
  93.3 0.6 copy-start
  142.7 3.7 %collective-permute-start.1 = (bf16[128,256]{1,0:T(8,128)(2,1)S(1)}, bf16[128,256]{1,0:T(8,128)(2,1)S(1)}, u32[]{:S(2)}, u32[]{:S(2)}) collective-permute-start(bf16[128,256]{1,0:T(8,128)(2,1)S(1)} %fusion.2), channel_id=1, source_target_pairs={{0,28},{4,0},{8,4},{12,8},{16,12},{20,16},{24,20},{28,24},{32,60},... | collective-permute-start | bytes 196616 | tf_op jit(solution)/shard_map/ppermute | solution.py:709
  146.4 0.6 copy-start.1

commit v2 on v0

v2 whole, which is shorter than its diff:
```python
import jax
import jax.numpy as jnp
import numpy as np
from jax import lax
from jax.experimental import pallas as pl
from jax.experimental.pallas import tpu as pltpu
from jax.sharding import PartitionSpec as P

HEADS = 8
HEAD_DIM = 128
SPAN = 128
TOK = 256
SLOT = 6
GRP = 8
CHUNK = GRP * SLOT
MSG = GRP * CHUNK
ROUNDS = 4
ROWS = GRP * TOK
NBLK = ROWS // SPAN
NEG = -1e30
SCALE = HEAD_DIM ** (-0.5)
f32 = jnp.float32
bf16 = jnp.bfloat16
i32 = jnp.int32
ANY = pl.ANY


def here():
    x = lax.axis_index("round")
    s = lax.axis_index("seq")
    return x, lax.div(s, GRP), lax.rem(s, GRP)


def device(x, z, k):
    return {"seq": z * GRP + k, "round": x}


def remote(src, dst, send, recv, target):
    return pltpu.make_async_remote_copy(
        src_ref=src, dst_ref=dst, send_sem=send, recv_sem=recv,
        device_id=target, device_id_type=pl.DeviceIdType.MESH,
    )


def signal(sem, target):
    pl.semaphore_signal(sem, inc=1, device_id=target, device_id_type=pl.DeviceIdType.MESH)


def loop(lo, hi, body):
    def go(i, c):
        body(i)
        return c

    lax.fori_loop(lo, hi, go, 0)


def row_onehot(idx, count):
    places = lax.broadcasted_iota(i32, (count, TOK), 0)
    return jnp.where(places == idx, 1.0, 0.0).astype(bf16)


def col_of(idx):
    wide = jnp.broadcast_to(idx.astype(f32), (128, TOK))
    return jnp.concatenate([wide[:, :128].T, wide[:, 128:].T], axis=0).astype(i32)


def dot(a, b):
    return jnp.dot(a, b, preferred_element_type=f32)


def dot_nt(a, b):
    return lax.dot_general(a, b, (((1,), (1,)), ((), ())), preferred_element_type=f32)


def dot_tn(a, b):
    return lax.dot_general(a, b, (((0,), (0,)), ((), ())), preferred_element_type=f32)


def three(a):
    hi = a.astype(bf16)
    left = a - hi.astype(f32)
    mid = left.astype(bf16)
    low = (left - mid.astype(f32)).astype(bf16)
    return hi.astype(f32), mid.astype(f32), low.astype(f32)


def window(rows, tail, b):
    own = rows[b]
    if isinstance(b, int) and b == 0:
        before = tail[...]
    else:
        before = rows[b - 1][:, HEAD_DIM:3 * HEAD_DIM]
    keys = jnp.concatenate([before[:, :HEAD_DIM], own[:, HEAD_DIM:2 * HEAD_DIM]], axis=0)
    vals = jnp.concatenate([before[:, HEAD_DIM:], own[:, 2 * HEAD_DIM:3 * HEAD_DIM]], axis=0)
    return own[:, :HEAD_DIM], keys, vals, own[:, 3 * HEAD_DIM:]


def cols(ref, h):
    return ref.at[:, pl.ds(pl.multiple_of(h * HEAD_DIM, HEAD_DIM), HEAD_DIM)]


def both(copy):
    copy.wait_send()
    copy.wait_recv()


def ranks(col, row, before):
    return jnp.sum(jnp.where(jnp.logical_and(col == row, before), 1.0, 0.0), axis=0, keepdims=True)


def wide_col(row):
    col = col_of(row)
    return jnp.concatenate([col, col], axis=1)


def whole_kernel(
    q, k_, v, g_, inv, ordr, bucket, swap, final,
    sidx, ridx, sall, rall, zin, packed, recv, table, ohr, ohrt, ohst, mid, rows, tail,
    stat, smid, sent, got, across, reply, back, bmid, outq, outkv, spill_out, spill_in,
    packed2, recv2, settled, near,
    zs, zr, ss, sr, rs, rr, ls, ps, pr, ts, tr, s1, r1, s2, r2, s3, r3, ws, wr, bs, br, hs, hr,
):
    x, z, k = here()
    line = x * GRP + z
    me = x * GRP + k
    total = 4 * GRP
    barrier = pltpu.get_barrier_semaphore()

    def on_line(i):
        o = lax.rem(line + i, total)
        return o, device(lax.div(o, GRP), lax.rem(o, GRP), k)

    def on_plane(i):
        o = lax.rem(me + i * 11, total)
        return o, device(lax.div(o, GRP), z, lax.rem(o, GRP))

    def greet(i):
        signal(barrier, on_line(i)[1])
        signal(barrier, on_plane(i)[1])

    loop(1, total, greet)
    mine = (z == k).astype(i32)

    def greet_pos(i):
        @pl.when(jnp.logical_or(z != k, i != z))
        def _():
            signal(barrier, device(x, i, z))

        @pl.when(jnp.logical_or(z != k, i != k))
        def _():
            signal(barrier, device(x, k, i))

    loop(0, GRP, greet_pos)

    for t, ref in enumerate((q, k_, v, g_)):
        @pl.when(x == t)
        def _(ref=ref):
            pltpu.make_async_copy(cols(ref, z), zin.at[z], ls.at[0]).start()

    up = lax.broadcasted_iota(i32, (TOK, TOK), 0)
    across_ = lax.broadcasted_iota(i32, (TOK, TOK), 1)
    target = lax.shift_right_logical(inv[...], 8)
    rank = ranks(wide_col(target), target, up < across_).astype(i32)
    sidx[...] = target * SLOT + rank
    tokens = ordr[...]
    source = lax.shift_right_logical(tokens, 8)
    rank = ranks(wide_col(source), source, wide_col(tokens) < tokens).astype(i32)
    part = jnp.bitwise_and(source, GRP - 1)
    ridx[...] = part * CHUNK + lax.shift_right_logical(source, 3) * SLOT + rank

    pl.semaphore_wait(barrier, 2 * (total - 1) + 2 * (GRP - mine))

    def send_idx(i):
        o, target_ = on_line(i)
        remote(sidx, sall.at[line], ss.at[o], sr.at[line], target_).start()

    loop(1, total, send_idx)
    sall[line] = sidx[...]

    for t, ref in enumerate((q, k_, v, g_)):
        @pl.when(x == t)
        def _(ref=ref):
            def go(i):
                step = lax.div(i + 1, 2)
                o = lax.rem(z + jnp.where(lax.rem(i, 2) == 1, step, GRP - step), GRP)
                remote(cols(ref, o), zin.at[z], zs.at[o], zr.at[z], device(x, o, k)).start()

            loop(1, GRP, go)

    def send_pos(i):
        @pl.when(jnp.logical_or(z != k, i != z))
        def _():
            remote(ridx, rall.at[k], rs.at[i], rr.at[k], device(x, i, z)).start()

    loop(0, GRP, send_pos)

    @pl.when(z == k)
    def _():
        rall[k] = ridx[...]

    def wait_idx(i):
        o, target_ = on_line(i)
        both(remote(sidx, sall.at[o], ss.at[o], sr.at[o], target_))

    loop(1, total, wait_idx)

    def pack_one(i):
        @pl.when(i == z)
        def _():
            pltpu.make_async_copy(cols(q, z), zin.at[z], ls.at[0]).wait()

        @pl.when(i != z)
        def _():
            both(remote(cols(q, i), zin.at[i], zs.at[i], zr.at[i], device(x, i, k)))

        def per_round(r):
            onehot = row_onehot(sall[r * GRP + i], MSG)
            value = dot(onehot, zin[i]).astype(bf16).reshape(GRP, CHUNK, HEAD_DIM)
            packed[pl.ds(r * GRP, GRP), i] = value

        loop(0, ROUNDS, per_round)

    def pack_pair(j):
        p = lax.rem(lax.div(z, 2) + j + lax.div(j, 2) - 2 * lax.div(j, 3), 4)
        pack_one(2 * p)
        pack_one(2 * p + 1)

        def go(i):
            o, target_ = on_plane(i)
            remote(packed.at[o, pl.ds(2 * p, 2)], recv.at[me, pl.ds(2 * p, 2)],
                   ps.at[o, p], pr.at[me, p], target_).start()

        loop(1, total, go)

    loop(0, 4, pack_pair)
    recv[me] = packed[me]

    def wait_pos(i):
        @pl.when(jnp.logical_or(z != k, i != z))
        def _():
            remote(ridx, rall.at[k], rs.at[i], rr.at[i], device(x, i, z)).wait_send()

        @pl.when(jnp.logical_or(z != k, i != k))
        def _():
            remote(ridx, rall.at[i], rs.at[i], rr.at[i], device(x, k, i)).wait_recv()

    loop(0, GRP, wait_pos)

    lanes = lax.broadcasted_iota(i32, (TOK, 128), 1)

    def fill_near(b):
        near[b] = bucket[lax.rem(k * NBLK + b + GRP * NBLK - 1, GRP * NBLK)].astype(f32)

    loop(0, NBLK + 1, fill_near)

    def fill_pos(d):
        col = col_of(rall[d])
        for m in range(3):
            ohr[d, :, m * 128:(m + 1) * 128] = jnp.where(col == lanes + m * 128, 1.0, 0.0).astype(bf16)
        ohrt[d] = row_onehot(rall[d], MSG)

    loop(0, GRP, fill_pos)

    def fill_tok(n):
        col = col_of(sall[n])
        for m in range(3):
            ohst[n, :, m * 128:(m + 1) * 128] = jnp.where(col == lanes + m * 128, 1.0, 0.0).astype(bf16)

    loop(0, total, fill_tok)

    def fill_table(i):
        table[:, i] = row_onehot(sall[x * GRP + i], MSG).reshape(GRP, CHUNK, TOK)

    loop(0, GRP, fill_table)

    def first(i):
        g = lax.rem(k + i, GRP)

        def arrived(n):
            t = lax.div(n, 4)
            p = lax.rem(n, 4)
            o = t * GRP + g

            @pl.when(o != me)
            def _():
                both(remote(packed.at[o, pl.ds(2 * p, 2)], recv.at[o, pl.ds(2 * p, 2)],
                            ps.at[o, p], pr.at[o, p], device(t, z, g)))

        loop(0, 16, arrived)
        parts = [recv[t * GRP + g].reshape(MSG, HEAD_DIM) for t in range(4)]
        moved = dot(swap[...], jnp.concatenate(parts, axis=1)).astype(bf16)
        mid[:, g] = moved.reshape(GRP, CHUNK, 4 * HEAD_DIM)

    loop(0, GRP, first)

    def second(d):
        value = dot(ohr[d], mid[d].reshape(MSG, 4 * HEAD_DIM)).astype(bf16)
        rows[pl.ds(2 * d, 2)] = value.reshape(2, SPAN, 4 * HEAD_DIM)

    second(GRP - 1)
    after = device(x, z, lax.rem(k + 1, GRP))
    before = device(x, z, lax.rem(k + GRP - 1, GRP))
    tail_copy = remote(rows.at[NBLK - 1, :, pl.ds(HEAD_DIM, 2 * HEAD_DIM)], tail, ts.at[0], tr.at[0],
                       after)
    tail_copy.start()
    loop(0, GRP - 1, second)

    def allowed_of(b):
        own = near[b + 1]
        col = jnp.broadcast_to(own, (SPAN, SPAN)).T
        return jnp.concatenate([col == near[b], col == own], axis=1)

    lane8 = jnp.bitwise_and(lax.broadcasted_iota(i32, (SPAN, 128), 1), 7)

    def forward(b):
        query, keys, vals, grad = window(rows, tail, b)
        allowed = allowed_of(b)
        scores = jnp.where(allowed, dot_nt(query, keys) * SCALE, NEG)
        peak = jnp.max(scores, axis=-1, keepdims=True)
        expon = jnp.where(allowed, jnp.exp(scores - peak), 0.0)
        norm = jnp.sum(expon, axis=-1, keepdims=True)
        output = dot((expon / norm).astype(bf16), vals)
        lse = peak + jnp.log(norm)
        inner = jnp.sum(output * grad.astype(f32), axis=-1, keepdims=True)
        value = jnp.zeros((SPAN, 128), f32)
        for n, piece in enumerate(three(lse) + three(inner)):
            value = jnp.where(lane8 == n, piece, value)
        stat[b] = value.astype(bf16)

    loop(1, NBLK, forward)
    both(tail_copy)
    forward(0)
    group = lax.shift_right_logical(lax.broadcasted_iota(i32, (CHUNK, 128), 1), 3)

    def stat_pack(d):
        moved = dot(ohrt[d], stat[pl.ds(2 * d, 2)].reshape(TOK, 128))
        value = jnp.zeros((CHUNK, 128), f32)
        for g in range(GRP):
            value = jnp.where(group == g, moved[g * CHUNK:(g + 1) * CHUNK], value)
        smid[d] = value.astype(bf16)

    loop(0, GRP, stat_pack)
    sent[...] = dot(swap[...], smid[...].reshape(MSG, 128)).T[:8 * GRP].reshape(GRP, 8, MSG)

    def on_k(i):
        o = lax.rem(k + i, GRP)
        return o, device(x, z, o)

    def on_x(i):
        o = lax.rem(x + i, ROUNDS)
        return o, device(o, z, k)

    def go1(i):
        o, target_ = on_k(i)
        remote(sent.at[o], got.at[k], s1.at[o], r1.at[k], target_).start()

    loop(1, GRP, go1)
    got[k] = sent[k]

    def end1(i):
        o, target_ = on_k(i)
        both(remote(sent.at[o], got.at[o], s1.at[o], r1.at[o], target_))

    loop(1, GRP, end1)
    place = lax.broadcasted_iota(i32, (8, MSG), 1)
    start = lax.broadcasted_iota(i32, (8, MSG), 0) * CHUNK
    keep = jnp.logical_and(place >= start, place < start + CHUNK)

    def collect(o, acc):
        piece = got[o]
        wide = [jnp.where(keep, jnp.broadcast_to(piece[n:n + 1], (8, MSG)), 0.0) for n in range(6)]
        return acc + dot(jnp.concatenate(wide, axis=0).astype(bf16), table[o].reshape(MSG, TOK))

    tok = lax.fori_loop(0, GRP, collect, jnp.zeros((48, TOK), f32))
    across[x, 0] = tok[0:8] + tok[8:16] + tok[16:24]
    across[x, 1] = tok[24:32] + tok[32:40] + tok[40:48]

    def go2(i):
        o, target_ = on_x(i)
        remote(across.at[x], across.at[x], s2.at[o], r2.at[x], target_).start()

    loop(1, ROUNDS, go2)

    def end2(i):
        o, target_ = on_x(i)
        both(remote(across.at[x], across.at[o], s2.at[o], r2.at[o], target_))

    loop(1, ROUNDS, end2)
    lses = [across[r, 0] for r in range(ROUNDS)]
    top = jnp.maximum(jnp.maximum(lses[0], lses[1]), jnp.maximum(lses[2], lses[3]))
    exps = [jnp.exp(a - top) for a in lses]
    norm = (exps[0] + exps[1]) + (exps[2] + exps[3])
    joint = top + jnp.log(norm)
    delta = sum(exps[r] * across[r, 1] for r in range(ROUNDS)) / norm
    pieces = jnp.concatenate(three(joint) + three(delta), axis=0).astype(bf16)

    def answer(o):
        wide = dot_nt(pieces, table[o].reshape(MSG, TOK))
        parts = [jnp.sum(jnp.where(keep, wide[n * 8:(n + 1) * 8], 0.0), axis=0, keepdims=True)
                 for n in range(6)]
        parts += [jnp.zeros((2, MSG), f32)]
        reply[o] = jnp.concatenate(parts, axis=0)

    loop(0, GRP, answer)

    def go3(i):
        o, target_ = on_k(i)
        remote(reply.at[o], back.at[k], s3.at[o], r3.at[k], target_).start()

    loop(1, GRP, go3)
    back[k] = reply[k]

    def end3(i):
        o, target_ = on_k(i)
        both(remote(reply.at[o], back.at[o], s3.at[o], r3.at[o], target_))

    loop(1, GRP, end3)
    flat = jnp.concatenate(
        [back[...].reshape(8 * GRP, MSG), jnp.zeros((128 - 8 * GRP, MSG), f32)], axis=0
    )
    bmid[...] = dot(swap[...], flat.T.astype(bf16)).astype(bf16).reshape(GRP, CHUNK, 128)
    lane_tok = jnp.bitwise_and(lanes, 7)

    def joint_of(d):
        part_ = bmid[d].astype(f32)
        wide = jnp.concatenate(
            [jnp.where(group == g, part_, 0.0) for g in range(GRP)], axis=0
        ).astype(bf16)
        found = dot(ohr[d], wide)
        lse = jnp.sum(jnp.where(lane_tok < 3, found, 0.0), axis=-1, keepdims=True)
        dlt = jnp.sum(jnp.where(jnp.logical_and(lane_tok >= 3, lane_tok < 6), found, 0.0),
                      axis=-1, keepdims=True)
        return lse, dlt

    outkv[0] = jnp.zeros((SPAN, 2 * HEAD_DIM), f32)

    def backward(b, lse, dlt):
        query, keys, vals, grad = window(rows, tail, b)
        allowed = allowed_of(b)
        scores = dot_nt(query, keys) * SCALE
        prob = jnp.exp(jnp.where(allowed, scores - lse, NEG))
        low = prob.astype(bf16)
        value_grad = dot_tn(low, grad)
        prob_grad = dot_nt(grad, vals)
        score_grad = (prob * (prob_grad - dlt)).astype(bf16)
        query_grad = dot(score_grad, keys) * SCALE
        key_grad = dot_tn(score_grad, query) * SCALE
        outq[b] = jnp.concatenate([dot(low, vals), query_grad], axis=1).astype(bf16)
        pair = jnp.concatenate([key_grad, value_grad], axis=1)
        outkv[b] = outkv[b] + pair[:SPAN]
        outkv[b + 1] = pair[SPAN:]

    def backward_pair(d):
        lse, dlt = joint_of(d)
        backward(2 * d, lse[:SPAN], dlt[:SPAN])
        backward(2 * d + 1, lse[SPAN:], dlt[SPAN:])

    backward_pair(0)
    spill_out[...] = outkv[0].astype(bf16)
    spill_copy = remote(spill_out, spill_in, ws.at[0], wr.at[0], before)
    spill_copy.start()
    loop(1, GRP, backward_pair)

    def repack(d):
        upper = jnp.concatenate([outq[2 * d], outkv[2 * d + 1].astype(bf16)], axis=1)
        lower = jnp.concatenate([outq[2 * d + 1], outkv[2 * d + 2].astype(bf16)], axis=1)
        moved = dot(ohrt[d], jnp.concatenate([upper, lower], axis=0)).astype(bf16)
        mid[:, d] = moved.reshape(GRP, CHUNK, 4 * HEAD_DIM)

    loop(0, GRP - 1, repack)
    both(spill_copy)
    outkv[NBLK] = outkv[NBLK] + spill_in[...].astype(f32)
    repack(GRP - 1)

    def reorder(g):
        moved = dot(swap[...], mid[g].reshape(MSG, 4 * HEAD_DIM)).astype(bf16)
        for i in range(GRP):
            for t in range(4):
                owner = lax.rem(t - i - z + 16, 4)
                packed2[owner * GRP + g, i] = moved[i * CHUNK:(i + 1) * CHUNK,
                                                    t * HEAD_DIM:(t + 1) * HEAD_DIM]

    loop(0, GRP, reorder)

    def back_pair(j):
        p = lax.rem(lax.div(z, 2) + j, 4)

        def go(i):
            o, target_ = on_plane(i)
            remote(packed2.at[o, pl.ds(2 * p, 2)], recv2.at[me, pl.ds(2 * p, 2)],
                   bs.at[o, p], br.at[me, p], target_).start()

        loop(1, total, go)

    loop(0, 4, back_pair)
    recv2[me] = packed2[me]
    owner = lax.div(z, 2)
    side = lax.rem(z, 2)

    def home(i, begin):
        kind = lax.rem(x + i + z, 4)

        @pl.when(kind == 0)
        def _():
            for o in range(ROUNDS):
                own = jnp.logical_and(x == o, z == i)

                @pl.when(jnp.logical_not(own))
                def _(o=o):
                    cp = remote(settled.at[i], final.at[z], hs.at[i, o], hr.at[z], device(o, i, k))
                    cp.start() if begin else cp.wait_send()

                @pl.when(own)
                def _():
                    cp = pltpu.make_async_copy(settled.at[i], final.at[z], ls.at[1])
                    cp.start() if begin else cp.wait()

        tile = GRP + 2 * (kind - 1) + side
        own = jnp.logical_and(x == owner, z == i)

        @pl.when(jnp.logical_and(kind != 0, jnp.logical_not(own)))
        def _():
            cp = remote(settled.at[i], final.at[tile], hs.at[i, 0], hr.at[tile], device(owner, i, k))
            cp.start() if begin else cp.wait_send()

        @pl.when(jnp.logical_and(kind != 0, own))
        def _():
            cp = pltpu.make_async_copy(settled.at[i], final.at[tile], ls.at[1])
            cp.start() if begin else cp.wait()

    def settle(i):
        acc = jnp.zeros((TOK, HEAD_DIM), f32)
        for r in range(ROUNDS):
            acc = acc + dot(ohst[r * GRP + i], recv2[r * GRP:(r + 1) * GRP, i].reshape(MSG, HEAD_DIM))
        settled[i] = acc.astype(bf16)
        home(i, True)

    def settle_pair(j):
        p = lax.rem(lax.div(z, 2) + j, 4)

        def end(i):
            o, target_ = on_plane(i)
            both(remote(packed2.at[o, pl.ds(2 * p, 2)], recv2.at[o, pl.ds(2 * p, 2)],
                        bs.at[o, p], br.at[o, p], target_))

        loop(1, total, end)
        loop(2 * p, 2 * p + 2, settle)

    loop(0, 4, settle_pair)
    loop(0, GRP, lambda i: home(i, False))

    def arrive(tile, kind, h):
        sender = lax.rem(32 + kind - z - h, 4)

        @pl.when(jnp.logical_not(jnp.logical_and(h == z, sender == x)))
        def _():
            remote(settled.at[0], final.at[tile], hs.at[0, 0], hr.at[tile],
                   device(sender, h, k)).wait_recv()

    loop(0, GRP, lambda h: arrive(h, 0, h))
    loop(0, 6, lambda n: arrive(GRP + n, 1 + lax.div(n, 2), 2 * x + lax.rem(n, 2)))


def whole(q, k, v, g, inv, ordr, bucket, swap):
    n = 4 * GRP
    dma = pltpu.SemaphoreType.DMA
    vm = pltpu.VMEM
    spec = pl.BlockSpec(memory_space=pltpu.VMEM)
    wide = 4 * HEAD_DIM
    return pl.pallas_call(
        whole_kernel,
        out_shape=jax.ShapeDtypeStruct((14, TOK, HEAD_DIM), bf16),
        in_specs=[pl.BlockSpec(memory_space=ANY)] * 4 + [spec] * 4,
        out_specs=pl.BlockSpec(memory_space=ANY),
        scratch_shapes=[
            vm((1, TOK), i32), vm((1, TOK), i32), vm((n, 1, TOK), i32), vm((GRP, 1, TOK), i32),
            vm((GRP, TOK, HEAD_DIM), bf16),
            vm((n, GRP, CHUNK, HEAD_DIM), bf16), vm((n, GRP, CHUNK, HEAD_DIM), bf16),
            vm((GRP, GRP, CHUNK, TOK), bf16), vm((GRP, TOK, MSG), bf16), vm((GRP, MSG, TOK), bf16),
            vm((n, TOK, MSG), bf16), vm((GRP, GRP, CHUNK, wide), bf16),
            vm((NBLK, SPAN, wide), bf16), vm((SPAN, 2 * HEAD_DIM), bf16),
            vm((NBLK, SPAN, 128), bf16), vm((GRP, CHUNK, 128), bf16),
            vm((GRP, 8, MSG), f32), vm((GRP, 8, MSG), f32), vm((ROUNDS, 2, GRP, TOK), f32),
            vm((GRP, 8, MSG), f32), vm((GRP, 8, MSG), f32), vm((GRP, CHUNK, 128), bf16),
            vm((NBLK, SPAN, 2 * HEAD_DIM), bf16), vm((NBLK + 1, SPAN, 2 * HEAD_DIM), f32),
            vm((SPAN, 2 * HEAD_DIM), bf16), vm((SPAN, 2 * HEAD_DIM), bf16),
            vm((n, GRP, CHUNK, HEAD_DIM), bf16), vm((n, GRP, CHUNK, HEAD_DIM), bf16),
            vm((GRP, TOK, HEAD_DIM), bf16), vm((NBLK + 1, 1, SPAN), f32),
            dma((GRP,)), dma((GRP,)), dma((n,)), dma((n,)), dma((GRP,)), dma((GRP,)), dma((2,)),
            dma((n, 4)), dma((n, 4)), dma((1,)), dma((1,)),
            dma((GRP,)), dma((GRP,)), dma((ROUNDS,)), dma((ROUNDS,)), dma((GRP,)), dma((GRP,)),
            dma((1,)), dma((1,)), dma((n, 4)), dma((n, 4)), dma((GRP, ROUNDS)), dma((14,)),
        ],
        compiler_params=pltpu.CompilerParams(
            collective_id=0, has_side_effects=True, vmem_limit_bytes=60 * 1024 * 1024
        ),
        name="whole",
    )(q, k, v, g, inv, ordr, bucket, swap)


def finish_kernel(tiles, att, gq, gk, gv):
    for h in range(HEADS):
        att[:, h * HEAD_DIM:(h + 1) * HEAD_DIM] = tiles[h]
    for t, ref in enumerate((gq, gk, gv)):
        for n in range(2):
            ref[:, n * HEAD_DIM:(n + 1) * HEAD_DIM] = tiles[GRP + 2 * t + n]


def finish(tiles):
    part = jax.ShapeDtypeStruct((TOK, 2 * HEAD_DIM), bf16)
    return pl.pallas_call(
        finish_kernel,
        out_shape=(jax.ShapeDtypeStruct((TOK, HEADS * HEAD_DIM), bf16), part, part, part),
        name="finish",
    )(tiles)


def swap_matrix():
    at = np.arange(MSG)
    mirror = (at // SLOT % GRP) * CHUNK + (at // CHUNK) * SLOT + at % SLOT
    return (mirror[:, None] == at[None, :]).astype(jnp.bfloat16)


def on_device(queries, keys, values, cotangent, order, inverse, bucket):
    return finish(whole(queries, keys, values, cotangent, inverse, order,
                        bucket.reshape(GRP * NBLK, 1, SPAN), jnp.asarray(swap_matrix())))


def solution(mesh):
    return jax.shard_map(
        on_device,
        mesh=mesh,
        in_specs=(
            P("seq", None), P("seq", None), P("seq", None), P("seq", None),
            P("round", "seq"), P("round", "seq"), P("round", None),
        ),
        out_specs=(P("seq", None), P("seq", "round"), P("seq", "round"), P("seq", "round")),
        check_vma=False,
    )
```

time: 539 us -> 169 us (0.31)
  the two profiles are of different devices: /device:TPU:8 before, /device:TPU:71 now
where the time goes in v2:
time: 169 us; the launch traced here: 168 us
  Pallas kernels  168 us (99%)
    pallas_call x1, Pallas kernels, whole(): pl.pallas_call(whole_kernel, out_shape=jax.ShapeDtypeStruct((14, TOK, HEA...  165 us

profile of v2, /device:TPU:71, one launch (start us, length us, event | category | flops | bytes accessed | tf_op | source)
XLA Modules:
  0.0 168.3 jit_solution(5978556496819143598)
XLA Ops:
  0.6 165.3 %whole.1.tiles = bf16[14,256,128]{2,1,0:T(8,128)(2,1)} custom-call(bf16[256,1024]{1,0:T(8,128)(2,1)} %q.1, bf16[256,1024]{1,0:T(8,128)(2,1)} %k_.1, bf16[256,1024]{1,0:T(8,128)(2,1)} %v.1, bf16[256,1024]{1,0:T(8,128)(2,1)} %g_.1, s32[1,256]{1,0:T(1,128)} %inv.1, s32[1,256]{1,0:T(1,128)} %ordr.1, s32[128,1,128]{2,1,0:T(1,128)} %bitcast.1, ...), custom_call_target="tpu_custom_call" | custom-call | tf_op jit(solution)/shard_map/whole/pallas_call | solution.py:570
  166.0 2.3 %finish.1 = (bf16[256,1024]{1,0:T(8,128)(2,1)}, bf16[256,256]{1,0:T(8,128)(2,1)}, bf16[256,256]{1,0:T(8,128)(2,1)}, bf16[256,256]{1,0:T(8,128)(2,1)}) custom-call(bf16[14,256,128]{2,1,0:T(8,128)(2,1)} %whole.1.tiles), custom_call_target="tpu_custom_call" | custom-call | tf_op jit(solution)/shard_map/finish/pallas_call | solution.py:611

commit v3 on v2

--- a/solution.py
+++ b/solution.py
@@ -117,7 +117,7 @@
     q, k_, v, g_, inv, ordr, bucket, swap, final,
     sidx, ridx, sall, rall, zin, packed, recv, table, ohr, ohrt, ohst, mid, rows, tail,
     stat, smid, sent, got, across, reply, back, bmid, outq, outkv, spill_out, spill_in,
-    packed2, recv2, settled, near,
+    packed2, recv2, settled, near, score, pgrad,
     zs, zr, ss, sr, rs, rr, ls, ps, pr, ts, tr, s1, r1, s2, r2, s3, r3, ws, wr, bs, br, hs, hr,
 ):
     x, z, k = here()
@@ -316,6 +316,7 @@
         query, keys, vals, grad = window(rows, tail, b)
         allowed = allowed_of(b)
         scores = jnp.where(allowed, dot_nt(query, keys) * SCALE, NEG)
+        score[b] = scores
         peak = jnp.max(scores, axis=-1, keepdims=True)
         expon = jnp.where(allowed, jnp.exp(scores - peak), 0.0)
         norm = jnp.sum(expon, axis=-1, keepdims=True)
@@ -327,7 +328,11 @@
             value = jnp.where(lane8 == n, piece, value)
         stat[b] = value.astype(bf16)
 
-    loop(1, NBLK, forward)
+    def forward_three(j):
+        for n in range(3):
+            forward(1 + 3 * j + n)
+
+    loop(0, 5, forward_three)
     both(tail_copy)
     forward(0)
     group = lax.shift_right_logical(lax.broadcasted_iota(i32, (CHUNK, 128), 1), 3)
@@ -356,6 +361,17 @@
 
     loop(1, GRP, go1)
     got[k] = sent[k]
+
+    def prob_grad_of(b):
+        _, _, vals, grad = window(rows, tail, b)
+        pgrad[b] = dot_nt(grad, vals)
+
+    def prob_grad_three(j):
+        for n in range(3):
+            prob_grad_of(1 + 3 * j + n)
+
+    prob_grad_of(0)
+    loop(0, 5, prob_grad_three)
 
     def end1(i):
         o, target_ = on_k(i)
@@ -436,13 +452,10 @@
 
     def backward(b, lse, dlt):
         query, keys, vals, grad = window(rows, tail, b)
-        allowed = allowed_of(b)
-        scores = dot_nt(query, keys) * SCALE
-        prob = jnp.exp(jnp.where(allowed, scores - lse, NEG))
+        prob = jnp.exp(score[b] - lse)
         low = prob.astype(bf16)
         value_grad = dot_tn(low, grad)
-        prob_grad = dot_nt(grad, vals)
-        score_grad = (prob * (prob_grad - dlt)).astype(bf16)
+        score_grad = (prob * (pgrad[b] - dlt)).astype(bf16)
         query_grad = dot(score_grad, keys) * SCALE
         key_grad = dot_tn(score_grad, query) * SCALE
         outq[b] = jnp.concatenate([dot(low, vals), query_grad], axis=1).astype(bf16)
@@ -586,6 +599,7 @@
             vm((SPAN, 2 * HEAD_DIM), bf16), vm((SPAN, 2 * HEAD_DIM), bf16),
             vm((n, GRP, CHUNK, HEAD_DIM), bf16), vm((n, GRP, CHUNK, HEAD_DIM), bf16),
             vm((GRP, TOK, HEAD_DIM), bf16), vm((NBLK + 1, 1, SPAN), f32),
+            vm((NBLK, SPAN, 2 * SPAN), f32), vm((NBLK, SPAN, 2 * SPAN), f32),
             dma((GRP,)), dma((GRP,)), dma((n,)), dma((n,)), dma((GRP,)), dma((GRP,)), dma((2,)),
             dma((n, 4)), dma((n, 4)), dma((1,)), dma((1,)),
             dma((GRP,)), dma((GRP,)), dma((ROUNDS,)), dma((ROUNDS,)), dma((GRP,)), dma((GRP,)),

time: 169 us -> 163 us (0.964)
  Pallas kernels: 168 us -> 162 us
    pallas_call x1, Pallas kernels: 165 us -> 160 us  [whole(): pl.pallas_call(whole_kernel, out_shape=jax.ShapeDtypeStruct((14, TOK, HEA...]
where the time goes in v3:
time: 163 us
  Pallas kernels  162 us (99%)
    pallas_call x1, Pallas kernels, whole(): pl.pallas_call(whole_kernel, out_shape=jax.ShapeDtypeStruct((14, TOK, HEA...  160 us

profile of v3, /device:TPU:71, one launch (start us, length us, event | category | flops | bytes accessed | tf_op | source)
XLA Modules:
  0.0 162.9 jit_solution(18006086330879951641)
XLA Ops:
  0.6 159.9 %whole.1.tiles = bf16[14,256,128]{2,1,0:T(8,128)(2,1)} custom-call(bf16[256,1024]{1,0:T(8,128)(2,1)} %q.1, bf16[256,1024]{1,0:T(8,128)(2,1)} %k_.1, bf16[256,1024]{1,0:T(8,128)(2,1)} %v.1, bf16[256,1024]{1,0:T(8,128)(2,1)} %g_.1, s32[1,256]{1,0:T(1,128)} %inv.1, s32[1,256]{1,0:T(1,128)} %ordr.1, s32[128,1,128]{2,1,0:T(1,128)} %bitcast.1, ...), custom_call_target="tpu_custom_call" | custom-call | tf_op jit(solution)/shard_map/whole/pallas_call | solution.py:583
  160.6 2.3 %finish.1 = (bf16[256,1024]{1,0:T(8,128)(2,1)}, bf16[256,256]{1,0:T(8,128)(2,1)}, bf16[256,256]{1,0:T(8,128)(2,1)}, bf16[256,256]{1,0:T(8,128)(2,1)}) custom-call(bf16[14,256,128]{2,1,0:T(8,128)(2,1)} %whole.1.tiles), custom_call_target="tpu_custom_call" | custom-call | tf_op jit(solution)/shard_map/finish/pallas_call | solution.py:625

commit v4 on v3

--- a/solution.py
+++ b/solution.py
@@ -54,6 +54,14 @@
     lax.fori_loop(lo, hi, go, 0)
 
 
+def pairs(count, body):
+    def go(i):
+        body(2 * i)
+        body(2 * i + 1)
+
+    loop(0, count // 2, go)
+
+
 def row_onehot(idx, count):
     places = lax.broadcasted_iota(i32, (count, TOK), 0)
     return jnp.where(places == idx, 1.0, 0.0).astype(bf16)
@@ -344,7 +352,7 @@
             value = jnp.where(group == g, moved[g * CHUNK:(g + 1) * CHUNK], value)
         smid[d] = value.astype(bf16)
 
-    loop(0, GRP, stat_pack)
+    pairs(GRP, stat_pack)
     sent[...] = dot(swap[...], smid[...].reshape(MSG, 128)).T[:8 * GRP].reshape(GRP, 8, MSG)
 
     def on_k(i):
@@ -387,7 +395,8 @@
         wide = [jnp.where(keep, jnp.broadcast_to(piece[n:n + 1], (8, MSG)), 0.0) for n in range(6)]
         return acc + dot(jnp.concatenate(wide, axis=0).astype(bf16), table[o].reshape(MSG, TOK))
 
-    tok = lax.fori_loop(0, GRP, collect, jnp.zeros((48, TOK), f32))
+    tok = lax.fori_loop(0, GRP // 2, lambda i, acc: collect(2 * i + 1, collect(2 * i, acc)),
+                        jnp.zeros((48, TOK), f32))
     across[x, 0] = tok[0:8] + tok[8:16] + tok[16:24]
     across[x, 1] = tok[24:32] + tok[32:40] + tok[40:48]
 
@@ -417,7 +426,7 @@
         parts += [jnp.zeros((2, MSG), f32)]
         reply[o] = jnp.concatenate(parts, axis=0)
 
-    loop(0, GRP, answer)
+    pairs(GRP, answer)
 
     def go3(i):
         o, target_ = on_k(i)

time: 163 us -> 161 us (0.988)
  Pallas kernels: 162 us -> 160 us
    pallas_call x1, Pallas kernels: 160 us -> 158 us  [whole(): pl.pallas_call(whole_kernel, out_shape=jax.ShapeDtypeStruct((14, TOK, HEA...]
where the time goes in v4:
time: 161 us
  Pallas kernels  160 us (99%)
    pallas_call x1, Pallas kernels, whole(): pl.pallas_call(whole_kernel, out_shape=jax.ShapeDtypeStruct((14, TOK, HEA...  158 us

profile of v4, /device:TPU:71, one launch (start us, length us, event | category | flops | bytes accessed | tf_op | source)
XLA Modules:
  0.0 161.0 jit_solution(10906405352003762672)
XLA Ops:
  0.6 158.1 %whole.1.tiles = bf16[14,256,128]{2,1,0:T(8,128)(2,1)} custom-call(bf16[256,1024]{1,0:T(8,128)(2,1)} %q.1, bf16[256,1024]{1,0:T(8,128)(2,1)} %k_.1, bf16[256,1024]{1,0:T(8,128)(2,1)} %v.1, bf16[256,1024]{1,0:T(8,128)(2,1)} %g_.1, s32[1,256]{1,0:T(1,128)} %inv.1, s32[1,256]{1,0:T(1,128)} %ordr.1, s32[128,1,128]{2,1,0:T(1,128)} %bitcast.1, ...), custom_call_target="tpu_custom_call" | custom-call | tf_op jit(solution)/shard_map/whole/pallas_call | solution.py:592
  158.7 2.3 %finish.1 = (bf16[256,1024]{1,0:T(8,128)(2,1)}, bf16[256,256]{1,0:T(8,128)(2,1)}, bf16[256,256]{1,0:T(8,128)(2,1)}, bf16[256,256]{1,0:T(8,128)(2,1)}) custom-call(bf16[14,256,128]{2,1,0:T(8,128)(2,1)} %whole.1.tiles), custom_call_target="tpu_custom_call" | custom-call | tf_op jit(solution)/shard_map/finish/pallas_call | solution.py:634
